TPU v7x, 32 devices: a whole 2x2x4 slice. The times are simulated.
32 devices in a mesh: dp: 4 (over y, x), fsdp: 8 (over z, core).
Axes of the slice: x: 2, y: 2, z: 4, core: 2. Of those that a mesh axis runs over, the one named last changes fastest.
Arguments:
- scenes_in: bfloat16 [32, 256, 1024], P(('dp', 'fsdp')), may hold values from -6 to 6
- scene_lengths: int32 [32], P(('dp', 'fsdp')), may hold values from 128 to 256, as said below
- cotangent: bfloat16 [32, 256, 1024], P(('dp', 'fsdp')), may hold values from -6 to 6
- qkv_weight: bfloat16 [1024, 3072], P('fsdp'), may hold values from -0.1875 to 0.1875
- out_weight: bfloat16 [1024, 1024], P('fsdp'), may hold values from -0.75 to 0.75
- up_weight: bfloat16 [1024, 4096], P('fsdp'), may hold values from -0.1875 to 0.1875
- down_weight: bfloat16 [4096, 1024], P('fsdp'), may hold values from -0.125 to 0.125
- gain_one: bfloat16 [1024], P('fsdp'), may hold values from 0.5 to 1.5
- bias_one: bfloat16 [1024], P('fsdp'), may hold values from -2 to 2
- gain_two: bfloat16 [1024], P('fsdp'), may hold values from 0.5 to 1.5
- bias_two: bfloat16 [1024], P('fsdp'), may hold values from -2 to 2
Outputs:
- layer_out: bfloat16 [32, 256, 1024], P(('dp', 'fsdp'))
- input_grad: bfloat16 [32, 256, 1024], P(('dp', 'fsdp'))
- qkv_grad: float32 [1024, 3072], P('fsdp')
- out_grad: float32 [1024, 1024], P('fsdp')
- up_grad: float32 [1024, 4096], P('fsdp')
- down_grad: float32 [4096, 1024], P('fsdp')
- gain_one_grad: float32 [1024], P('fsdp')
- bias_one_grad: float32 [1024], P('fsdp')
- gain_two_grad: float32 [1024], P('fsdp')
- bias_two_grad: float32 [1024], P('fsdp')
Inputs may be any that keep to these rules, and one draw needn't show every extreme that they name: `scene_lengths`: each length is a multiple of 128; some scene has exactly 256 tokens.
All inputs are finite; a program needn't handle non-finite values.
Results may differ from a plain program's by a relative error of at most 0.017.
Values may be sent and summed in bfloat16 or wider, within the bound.
A program may use at most 192 MiB of HBM per device.

v0:
```python
import math

import jax
import jax.numpy as jnp
from jax import lax
from jax.sharding import PartitionSpec as P

D = 1024
HEADS = 16
HEAD_DIM = 64


epsilon = 1e-05


def norm_rows(values_in):
    row_mean = jnp.mean(values_in, axis=-1, keepdims=True)
    centered = values_in - row_mean
    variance = jnp.mean(centered * centered, axis=-1, keepdims=True)
    inverse = lax.rsqrt(variance + epsilon)
    return (centered * inverse, inverse)


def norm_back(grad_normed, normed, inverse):
    first_mean = jnp.mean(grad_normed, axis=-1, keepdims=True)
    second_mean = jnp.mean(grad_normed * normed, axis=-1, keepdims=True)
    return inverse * (grad_normed - first_mean - normed * second_mean)


def inner_rows(left, right):
    return lax.dot_general(
        left, right, (((0,), (0,)), ((), ())), preferred_element_type=jnp.float32
    )


def outer_cols(left, right):
    return lax.dot_general(
        left, right, (((1,), (1,)), ((), ())), preferred_element_type=jnp.float32
    )


def forward_pass(inputs, key_valid, params):
    qkv_weight, out_weight, up_weight, down_weight, gain_one, bias_one, gain_two, bias_two = params
    seq_len = inputs.shape[0]
    normed_one, inverse_one = norm_rows(inputs)
    hidden_one = (normed_one * gain_one.astype(jnp.float32) + bias_one.astype(jnp.float32)).astype(
        jnp.bfloat16
    )
    qkv_low = jnp.dot(hidden_one, qkv_weight, preferred_element_type=jnp.float32).astype(
        jnp.bfloat16
    )
    split_view = qkv_low.reshape(seq_len, 3, HEADS, HEAD_DIM)
    queries = split_view[:, 0]
    keys_all = split_view[:, 1]
    values_all = split_view[:, 2]
    scale_factor = 1.0 / math.sqrt(HEAD_DIM)
    scores = (
        jnp.einsum("qhd,khd->hqk", queries, keys_all, preferred_element_type=jnp.float32)
        * scale_factor
    )
    masked = jnp.where(key_valid[None, None, :], scores, -1e30)
    highest = jnp.max(masked, axis=-1, keepdims=True)
    expont = jnp.exp(masked - highest)
    probs = expont / jnp.sum(expont, axis=-1, keepdims=True)
    probs_low = probs.astype(jnp.bfloat16)
    attended = jnp.einsum("hqk,khd->qhd", probs_low, values_all, preferred_element_type=jnp.float32)
    attn_low = attended.reshape(seq_len, D).astype(jnp.bfloat16)
    resid_one = inputs + jnp.dot(attn_low, out_weight, preferred_element_type=jnp.float32)
    normed_two, inverse_two = norm_rows(resid_one)
    hidden_two = (normed_two * gain_two.astype(jnp.float32) + bias_two.astype(jnp.float32)).astype(
        jnp.bfloat16
    )
    hidden_pre = jnp.dot(hidden_two, up_weight, preferred_element_type=jnp.float32)
    activated = jax.nn.gelu(hidden_pre, approximate=False).astype(jnp.bfloat16)
    result = resid_one + jnp.dot(activated, down_weight, preferred_element_type=jnp.float32)
    return (
        result,
        normed_one,
        inverse_one,
        hidden_one,
        queries,
        keys_all,
        values_all,
        probs,
        probs_low,
        attn_low,
        normed_two,
        inverse_two,
        hidden_two,
        hidden_pre,
        activated,
    )


def mlp_back(grad_out, saved, params):
    up_weight, down_weight, gain_two = (params[2], params[3], params[6])
    normed_two, inverse_two, hidden_two, hidden_pre, activated = (
        saved[10],
        saved[11],
        saved[12],
        saved[13],
        saved[14],
    )
    grad_low = grad_out.astype(jnp.bfloat16)
    down_grad = inner_rows(activated, grad_low)
    grad_act = outer_cols(grad_low, down_weight)
    cumul = 0.5 * (1.0 + lax.erf(hidden_pre * (1.0 / math.sqrt(2.0))))
    density = jnp.exp(-0.5 * hidden_pre * hidden_pre) * (1.0 / math.sqrt(2.0 * math.pi))
    grad_pre = (grad_act * (cumul + hidden_pre * density)).astype(jnp.bfloat16)
    up_grad = inner_rows(hidden_two, grad_pre)
    grad_hidden = outer_cols(grad_pre, up_weight)
    gain_two_grad = jnp.sum(grad_hidden * normed_two, axis=0)
    bias_two_grad = jnp.sum(grad_hidden, axis=0)
    grad_resid = grad_out + norm_back(
        grad_hidden * gain_two.astype(jnp.float32), normed_two, inverse_two
    )
    return (grad_resid, up_grad, down_grad, gain_two_grad, bias_two_grad)


def attn_back(grad_resid, saved, params):
    qkv_weight, out_weight, gain_one = (params[0], params[1], params[4])
    normed_one, inverse_one, hidden_one = (saved[1], saved[2], saved[3])
    queries, keys_all, values_all, probs, probs_low, attn_low = (
        saved[4],
        saved[5],
        saved[6],
        saved[7],
        saved[8],
        saved[9],
    )
    seq_len = grad_resid.shape[0]
    scale_factor = 1.0 / math.sqrt(HEAD_DIM)
    resid_low = grad_resid.astype(jnp.bfloat16)
    out_grad = inner_rows(attn_low, resid_low)
    grad_attn = (
        outer_cols(resid_low, out_weight).astype(jnp.bfloat16).reshape(seq_len, HEADS, HEAD_DIM)
    )
    grad_probs = jnp.einsum(
        "qhd,khd->hqk", grad_attn, values_all, preferred_element_type=jnp.float32
    )
    row_dot = jnp.sum(probs * grad_probs, axis=-1, keepdims=True)
    grad_scores = (probs * (grad_probs - row_dot)).astype(jnp.bfloat16)
    grad_values = jnp.einsum(
        "hqk,qhd->khd", probs_low, grad_attn, preferred_element_type=jnp.float32
    )
    grad_queries = (
        jnp.einsum("hqk,khd->qhd", grad_scores, keys_all, preferred_element_type=jnp.float32)
        * scale_factor
    )
    grad_keys = (
        jnp.einsum("hqk,qhd->khd", grad_scores, queries, preferred_element_type=jnp.float32)
        * scale_factor
    )
    grad_qkv = (
        jnp.stack([grad_queries, grad_keys, grad_values], axis=1)
        .reshape(seq_len, 3 * D)
        .astype(jnp.bfloat16)
    )
    qkv_grad = inner_rows(hidden_one, grad_qkv)
    grad_hidden = outer_cols(grad_qkv, qkv_weight)
    gain_one_grad = jnp.sum(grad_hidden * normed_one, axis=0)
    bias_one_grad = jnp.sum(grad_hidden, axis=0)
    input_grad = grad_resid + norm_back(
        grad_hidden * gain_one.astype(jnp.float32), normed_one, inverse_one
    )
    return (input_grad, qkv_grad, out_grad, gain_one_grad, bias_one_grad)


def on_device(
    scenes_in,
    scene_lengths,
    cotangent,
    qkv_weight,
    out_weight,
    up_weight,
    down_weight,
    gain_one,
    bias_one,
    gain_two,
    bias_two,
):
    params = (
        lax.all_gather(qkv_weight, "fsdp", axis=0, tiled=True),
        lax.all_gather(out_weight, "fsdp", axis=0, tiled=True),
        lax.all_gather(up_weight, "fsdp", axis=0, tiled=True),
        lax.all_gather(down_weight, "fsdp", axis=0, tiled=True),
        lax.all_gather(gain_one, "fsdp", axis=0, tiled=True),
        lax.all_gather(bias_one, "fsdp", axis=0, tiled=True),
        lax.all_gather(gain_two, "fsdp", axis=0, tiled=True),
        lax.all_gather(bias_two, "fsdp", axis=0, tiled=True),
    )
    inputs = scenes_in[0].astype(jnp.float32)
    seq_len = inputs.shape[0]
    positions = jnp.arange(seq_len, dtype=jnp.int32)
    key_valid = positions < scene_lengths[0]
    row_mask = key_valid.astype(jnp.float32)[:, None]
    saved = forward_pass(inputs, key_valid, params)
    layer_out = (saved[0] * row_mask).astype(jnp.bfloat16)[None]
    grad_out = cotangent[0].astype(jnp.float32) * row_mask
    params_back = (
        lax.all_gather(qkv_weight, "fsdp", axis=0, tiled=True),
        lax.all_gather(out_weight, "fsdp", axis=0, tiled=True),
        lax.all_gather(up_weight, "fsdp", axis=0, tiled=True),
        lax.all_gather(down_weight, "fsdp", axis=0, tiled=True),
        lax.all_gather(gain_one, "fsdp", axis=0, tiled=True),
        lax.all_gather(bias_one, "fsdp", axis=0, tiled=True),
        lax.all_gather(gain_two, "fsdp", axis=0, tiled=True),
        lax.all_gather(bias_two, "fsdp", axis=0, tiled=True),
    )
    saved_back = forward_pass(inputs, key_valid, params_back)
    grad_resid, up_grad, down_grad, gain_two_grad, bias_two_grad = mlp_back(
        grad_out, saved_back, params_back
    )
    input_grad, qkv_grad, out_grad, gain_one_grad, bias_one_grad = attn_back(
        grad_resid, saved_back, params_back
    )
    shares = (
        lax.psum_scatter(qkv_grad, "fsdp", scatter_dimension=0, tiled=True),
        lax.psum_scatter(out_grad, "fsdp", scatter_dimension=0, tiled=True),
        lax.psum_scatter(up_grad, "fsdp", scatter_dimension=0, tiled=True),
        lax.psum_scatter(down_grad, "fsdp", scatter_dimension=0, tiled=True),
        lax.psum_scatter(gain_one_grad, "fsdp", scatter_dimension=0, tiled=True),
        lax.psum_scatter(bias_one_grad, "fsdp", scatter_dimension=0, tiled=True),
        lax.psum_scatter(gain_two_grad, "fsdp", scatter_dimension=0, tiled=True),
        lax.psum_scatter(bias_two_grad, "fsdp", scatter_dimension=0, tiled=True),
    )
    summed = (
        lax.psum(shares[0].astype(jnp.bfloat16), "dp").astype(jnp.float32),
        lax.psum(shares[1].astype(jnp.bfloat16), "dp").astype(jnp.float32),
        lax.psum(shares[2].astype(jnp.bfloat16), "dp").astype(jnp.float32),
        lax.psum(shares[3].astype(jnp.bfloat16), "dp").astype(jnp.float32),
        lax.psum(shares[4].astype(jnp.bfloat16), "dp").astype(jnp.float32),
        lax.psum(shares[5].astype(jnp.bfloat16), "dp").astype(jnp.float32),
        lax.psum(shares[6].astype(jnp.bfloat16), "dp").astype(jnp.float32),
        lax.psum(shares[7].astype(jnp.bfloat16), "dp").astype(jnp.float32),
    )
    qkv_total, out_total, up_total, down_total = (summed[0], summed[1], summed[2], summed[3])
    gain_one_total, bias_one_total, gain_two_total, bias_two_total = (
        summed[4],
        summed[5],
        summed[6],
        summed[7],
    )
    input_out = input_grad.astype(jnp.bfloat16)[None]
    return (
        layer_out,
        input_out,
        qkv_total,
        out_total,
        up_total,
        down_total,
        gain_one_total,
        bias_one_total,
        gain_two_total,
        bias_two_total,
    )


def solution(mesh):
    placed = (
        P(("dp", "fsdp"), None, None),
        P(("dp", "fsdp")),
        P(("dp", "fsdp"), None, None),
        P("fsdp", None),
        P("fsdp", None),
        P("fsdp", None),
        P("fsdp", None),
        P("fsdp"),
        P("fsdp"),
        P("fsdp"),
        P("fsdp"),
    )
    return jax.shard_map(
        on_device,
        mesh=mesh,
        in_specs=placed,
        out_specs=(
            P(("dp", "fsdp"), None, None),
            P(("dp", "fsdp"), None, None),
            P("fsdp", None),
            P("fsdp", None),
            P("fsdp", None),
            P("fsdp", None),
            P("fsdp"),
            P("fsdp"),
            P("fsdp"),
            P("fsdp"),
        ),
        check_vma=False,
    )
```

profile of v0, /device:TPU:0, one launch (start us, length us, event | category | flops | bytes accessed | tf_op | source)
XLA Modules:
  0.0 905.0 jit_solution(12101224661716060638)
XLA Ops:
  7.2 0.7 all-gather.9.cloned.1.call-update
  8.0 0.7 all-gather.11.cloned.1.call-update
  8.7 0.7 all-gather.13.cloned.1.call-update
  9.5 0.5 all-gather.15.cloned.1.call-update
  10.0 13.6 %all-gather = bf16[8,1,128]{2,1,0:T(2,128)(2,1)S(1)} all-gather(bf16[1,1,128]{2,1,0:T(2,128)(2,1)} %bitcast.139), channel_id=1, replica_groups=mesh['dp'=4,'fsdp'=8] {'fsdp'}, dimensions={0}, use_global_device_ids=true | all-gather | bytes 2304 | tf_op jit(solution)/shard_map/all_gather | solution.py:187
  23.7 9.3 %all-gather.1 = bf16[8,1,128]{2,1,0:T(2,128)(2,1)S(1)} all-gather(bf16[1,1,128]{2,1,0:T(2,128)(2,1)} %bitcast.140), channel_id=1, replica_groups=mesh['dp'=4,'fsdp'=8] {'fsdp'}, dimensions={0}, use_global_device_ids=true | all-gather | bytes 2304 | tf_op jit(solution)/shard_map/all_gather | solution.py:188
  33.6 11.4 %all-gather.2 = bf16[8,1,128]{2,1,0:T(2,128)(2,1)S(1)} all-gather(bf16[1,1,128]{2,1,0:T(2,128)(2,1)} %bitcast.141), channel_id=1, replica_groups=mesh['dp'=4,'fsdp'=8] {'fsdp'}, dimensions={0}, use_global_device_ids=true | all-gather | bytes 2304 | tf_op jit(solution)/shard_map/all_gather | solution.py:189
  45.0 9.3 %all-gather.3 = bf16[8,1,128]{2,1,0:T(2,128)(2,1)S(1)} all-gather(bf16[1,1,128]{2,1,0:T(2,128)(2,1)} %bitcast.142), channel_id=1, replica_groups=mesh['dp'=4,'fsdp'=8] {'fsdp'}, dimensions={0}, use_global_device_ids=true | all-gather | bytes 2304 | tf_op jit(solution)/shard_map/all_gather | solution.py:190
  54.4 1.2 convert_reduce_fusion
  55.6 1.3 fusion.40
  56.9 20.2 %all-gather.9.cloned.1.call-done = bf16[1024,3072]{1,0:T(8,128)(2,1)} async-done(((bf16[128,3072]{1,0:T(8,128)(2,1)}), bf16[1024,3072]{1,0:T(8,128)(2,1)}) %all-gather.9.cloned.1.call-update) | async-done | bytes 6291472 | tf_op jit(solution)/shard_map/all_gather | solution.py:183
  77.1 5.8 convolution_convert_fusion
  82.9 1.7 copy.36
  84.7 0.7 fusion.63
  85.4 1.7 fusion.75
  87.2 2.0 copy-done.4
  89.1 0.5 convolution_convert_fusion.2
  89.7 16.8 %all-gather.11.cloned.1.call-done = bf16[1024,1024]{1,0:T(8,128)(2,1)} async-done(((bf16[128,1024]{1,0:T(8,128)(2,1)}), bf16[1024,1024]{1,0:T(8,128)(2,1)}) %all-gather.11.cloned.1.call-update) | async-done | bytes 2097168 | tf_op jit(solution)/shard_map/all_gather | solution.py:184
  106.5 2.4 fusion.76
  109.2 80.4 %all-gather.13.cloned.1.call-done = bf16[1024,4096]{1,0:T(8,128)(2,1)} async-done(((bf16[128,4096]{1,0:T(8,128)(2,1)}), bf16[1024,4096]{1,0:T(8,128)(2,1)}) %all-gather.13.cloned.1.call-update) | async-done | bytes 8388624 | tf_op jit(solution)/shard_map/all_gather | solution.py:185
  189.6 15.3 %fusion.4 = (bf16[256,4096]{1,0:T(8,128)(2,1)}, f32[256,4096]{1,0:T(8,128)}) fusion(bf16[1024,4096]{1,0:T(8,128)(2,1)} %all-gather.13.cloned.1.call-done, f32[256,1024]{1,0:T(8,128)S(1)} %get-tuple-element.33, f32[1024]{0:T(1024)S(1)} %bitcast.131, f32[1024]{0:T(1024)S(1)} %bitcast.127, f32[256]{0:T(256)S(1)} %add_rsqrt_fusion, ...), kind=kOutput, calls=%fused_computation.7 | convolution fusion | flops 2216951808 | bytes 15738880 | tf_op jit(solution)/shard_map/dot_general | solution.py:73
  204.8 66.8 %all-gather.15.cloned.1.call-done = bf16[4096,1024]{1,0:T(8,128)(2,1)} async-done(((bf16[512,1024]{1,0:T(8,128)(2,1)}), bf16[4096,1024]{1,0:T(8,128)(2,1)}) %all-gather.15.cloned.1.call-update) | async-done | bytes 8388624 | tf_op jit(solution)/shard_map/all_gather | solution.py:186
  271.6 6.8 fusion.1
  278.6 2.7 multiply_reduce_fusion.1
  281.3 0.4 fusion.45
  281.8 2.8 fusion.64
  284.6 2.3 convolution_convert_fusion.1
  287.0 1.0 copy.38
  288.0 3.8 multiply_reduce_fusion
  291.8 0.3 copy-done.5
  292.1 0.9 multiply_convert_fusion
  293.0 0.5 copy-done.2
  293.5 0.5 fusion.21
  294.0 0.8 fusion.20
  294.8 0.8 convolution_bitcast_fusion
  295.8 1.1 copy-done.3
  296.9 6.5 fusion.50
  303.5 0.3 reduce-scatter.9.cloned.1.call-start
  303.8 9.9 %fusion.73 = f32[1024,4096]{1,0:T(8,128)} fusion(bf16[256,4096]{1,0:T(8,128)(2,1)} %copy-done.10, f32[256,1024]{1,0:T(8,128)S(1)} %get-tuple-element.33, f32[1024]{0:T(1024)S(1)} %bitcast.132, f32[1024]{0:T(1024)S(1)} %bitcast.130, f32[256]{0:T(256)S(1)} %add_rsqrt_fusion, f32[256]{0:T(256)S(1)} %broadcast_multiply_fusion.4), kind=kOutput, calls=%fused_computation.121 | convolution fusion | flops 2148794368 | bytes 19933184 | tf_op jit(solution)/shard_map/dot_general | solution.py:31
  313.7 1.0 copy-done.7
  314.7 9.8 %fusion.67 = f32[4096,1024]{1,0:T(8,128)} fusion(bf16[256,4096]{1,0:T(8,128)(2,1)} %get-tuple-element.34, bf16[1,256,1024]{2,1,0:T(8,128)(2,1)S(1)} %copy-done.7, f32[256]{0:T(256)S(1)} %fusion.72), kind=kOutput, calls=%fused_computation.104 | convolution fusion | flops 2148270080 | bytes 19399680 | tf_op jit(solution)/shard_map/dot_general | solution.py:31
  324.6 8.6 reduce-scatter.7.cloned.1.call-done
  333.2 1.8 convert_element_type.185
  334.9 128.0 %reduce-scatter.5.cloned.1.call-done = f32[128,3072]{1,0:T(8,128)} async-done(((f32[1024,3072]{1,0:T(8,128)}), f32[128,3072]{1,0:T(8,128)}) %reduce-scatter.5.cloned.1.call-update) | async-done | bytes 1572880 | tf_op jit(solution)/shard_map/reduce_scatter | solution.py:218
  462.9 2.4 convert_element_type.183
  465.4 166.6 %reduce-scatter.9.cloned.1.call-done = f32[128,4096]{1,0:T(8,128)} async-done(((f32[1024,4096]{1,0:T(8,128)}), f32[128,4096]{1,0:T(8,128)}) %reduce-scatter.9.cloned.1.call-update) | async-done | bytes 2097168 | tf_op jit(solution)/shard_map/reduce_scatter | solution.py:220
  632.0 2.7 convert_element_type.187
  634.7 166.3 %reduce-scatter.11.cloned.1.call-done = f32[512,1024]{1,0:T(8,128)} async-done(((f32[4096,1024]{1,0:T(8,128)}), f32[512,1024]{1,0:T(8,128)}) %reduce-scatter.11.cloned.1.call-update) | async-done | bytes 2097168 | tf_op jit(solution)/shard_map/reduce_scatter | solution.py:221
  801.0 2.7 convert_element_type.189
  803.7 0.6 dynamic-slice
  805.0 6.3 fusion.39
  811.2 25.9 %all-reduce.4 = (bf16[1024]{0:T(1024)(128)(2,1)S(1)}, bf16[1024]{0:T(1024)(128)(2,1)S(1)}, bf16[1024]{0:T(1024)(128)(2,1)S(1)}, bf16[1024]{0:T(1024)(128)(2,1)S(1)}) all-reduce(f32[1024]{0:T(1024)S(1)} %get-tuple-element.12, f32[1024]{0:T(1024)S(1)} %get-tuple-element.17, ...), channel_id=6, replica_groups=mesh['dp'=4,'fsdp'=8] {'fsdp'}, use_global_device_ids=true, to_apply=%region_20.21.clone | all-reduce | flops 4096 | bytes 24576
  837.5 10.2 %all-reduce.5 = (bf16[128]{0:T(256)(128)(2,1)S(1)}, bf16[128]{0:T(256)(128)(2,1)S(1)}, bf16[128]{0:T(256)(128)(2,1)S(1)}, bf16[128]{0:T(256)(128)(2,1)S(1)}) all-reduce(bf16[128]{0:T(256)(128)(2,1)S(1)} %dynamic-slice.15, bf16[128]{0:T(256)(128)(2,1)S(1)} %dynamic-slice.14, ...), channel_id=1, replica_groups=mesh['dp'=4,'fsdp'=8] {'dp'}, use_global_device_ids=true, to_apply=%region_21.22 | all-reduce | flops 512 | bytes 2048 | tf_op jit(solution)/shard_map/psum | solution.py:232
  847.7 0.5 convert_element_type.192
  848.2 0.5 convert_element_type.194
  848.7 0.5 convert_element_type.196
  849.2 0.5 convert_element_type.198
  849.7 2.4 fusion.52
  852.2 7.8 fusion.31
  860.0 30.7 %all-reduce.9.cloned.1.call-done = (bf16[128,3072]{1,0:T(8,128)(2,1)}, bf16[128,1024]{1,0:T(8,128)(2,1)}, bf16[128,4096]{1,0:T(8,128)(2,1)}, bf16[512,1024]{1,0:T(8,128)(2,1)}) async-done(((bf16[128,3072]{1,0:T(8,128)(2,1)}, bf16[128,1024]{1,0:T(8,128)(2,1)}, bf16[128,4096]{1,0:T(8,128)(2,1)}, bf16[512,1024]{1,0:T(8,128)(2,1)}), (bf16[128,3072]{1,0:T(8,128)(2,1)}, bf16[128,1024]{1,0:T(8,128)(2,1)}, ...) | async-done | bytes 3145744 | tf_op jit(solution)/shard_map/psum | solution.py:228
  890.7 2.8 convert_element_type.188
  893.5 2.8 convert_element_type.190
  896.3 1.3 convert_element_type.184
  897.6 0.8 convert_element_type.186
  (59 shorter events, 1.5 us)
Async XLA Ops:
  7.2 69.9 %copy-start = (bf16[1,256,1024]{2,1,0:T(8,128)(2,1)S(1)}, bf16[1,256,1024]{2,1,0:T(8,128)(2,1)}, u32[]{:S(2)}) copy-start(bf16[1,256,1024]{2,1,0:T(8,128)(2,1)} %param.11) | copy-start | bytes 1572868
  7.2 69.9 %all-gather.9.cloned.1.call-start = ((), (), s32[]{:S(2)}) async-start(), calls=%async_computation.4 | async-start | bytes 7077888 | tf_op jit(solution)/shard_map/all_gather | solution.py:183
  7.9 98.6 %all-gather.11.cloned.1.call-start = ((), (), s32[]{:S(2)}) async-start(), calls=%async_computation.5 | async-start | bytes 2359296 | tf_op jit(solution)/shard_map/all_gather | solution.py:184
  8.7 180.9 %all-gather.13.cloned.1.call-start = ((), (), s32[]{:S(2)}) async-start(), calls=%async_computation.6 | async-start | bytes 9437184 | tf_op jit(solution)/shard_map/all_gather | solution.py:185
  9.4 262.2 %all-gather.15.cloned.1.call-start = ((), (), s32[]{:S(2)}) async-start(), calls=%async_computation.7 | async-start | bytes 9437184 | tf_op jit(solution)/shard_map/all_gather | solution.py:186
  10.0 323.2 %reduce-scatter.7.cloned.1.call-start = ((), (), s32[]{:S(2)}) async-start(), calls=%async_computation.9 | async-start | bytes 4718592 | tf_op jit(solution)/shard_map/reduce_scatter | solution.py:219
  84.7 2.5 copy-start.1
  87.2 2.0 copy-start.4
  89.6 115.2 %copy-start.8 = (bf16[16,64,256]{2,1,0:T(8,128)(2,1)}, bf16[16,64,256]{2,1,0:T(8,128)(2,1)S(1)}, u32[]{:S(2)}) copy-start(bf16[16,64,256]{2,1,0:T(8,128)(2,1)S(1)} %convolution_convert_fusion.2) | copy-start | bytes 1572868
  189.6 82.0 %copy-start.6 = (bf16[1,256,1024]{2,1,0:T(8,128)(2,1)S(1)}, bf16[1,256,1024]{2,1,0:T(8,128)(2,1)}, u32[]{:S(2)}) copy-start(bf16[1,256,1024]{2,1,0:T(8,128)(2,1)} %param.13) | copy-start | bytes 1572868
  271.6 7.0 copy-start.14
  278.6 2.7 copy-start.10
  278.6 3.1 copy-start.9
  284.6 178.4 %reduce-scatter.5.cloned.1.call-start = ((), (), s32[]{:S(2)}) async-start(), calls=%async_computation.8 | async-start | bytes 14155776 | tf_op jit(solution)/shard_map/reduce_scatter | solution.py:218
  288.0 4.1 copy-start.5
  292.1 1.4 copy-start.2
  293.5 1.2 copy-start.12
  295.8 1.1 copy-start.3
  303.5 328.5 %reduce-scatter.9.cloned.1.call-start = ((), (), s32[]{:S(2)}) async-start(), calls=%async_computation.10 | async-start | bytes 18874368 | tf_op jit(solution)/shard_map/reduce_scatter | solution.py:220
  313.7 1.0 copy-start.7
  313.7 487.3 %reduce-scatter.11.cloned.1.call-start = ((), (), s32[]{:S(2)}) async-start(), calls=%async_computation.11 | async-start | bytes 18874368 | tf_op jit(solution)/shard_map/reduce_scatter | solution.py:221
  324.6 566.1 %all-reduce.9.cloned.1.call-start = ((), (), s32[]{:S(2)}) async-start(), calls=%async_computation.12 | async-start | bytes 6291456 | tf_op jit(solution)/shard_map/psum | solution.py:228
  465.4 338.4 %copy-start.15 = (u32[32]{0:T(128)S(1)}, u32[32]{0:T(128)}, u32[]{:S(2)}) copy-start(u32[32]{0:T(128)} %constant.89) | copy-start | bytes 388
  890.7 5.6 copy-start.11
  890.7 6.9 copy-start.13
Sparse Core Ops, SparseCore 0:
  9.6 67.4 all-gather.8
  78.7 27.7 all-gather.10
  108.1 81.4 all-gather.12
  191.0 80.5 all-gather.14
  284.7 48.4 reduce-scatter.6
  335.3 127.5 reduce-scatter.4
  465.3 166.6 reduce-scatter.8
  634.3 166.6 reduce-scatter.10
  804.9 85.7 all-reduce.8
where the time goes:
time: 906 us; the launch traced here: 905 us
  waiting for transfers between devices  687 us (76%)
  matrix products  85.6 us (9%)
  blocking collectives  79.8 us (9%)
  other arithmetic  27.9 us (3%)
  between operations  15.4 us (2%)
    reduce_scatter x1, waiting for transfers between devices, on_device(): lax.psum_scatter(up_grad, 'fsdp', scatter_dimension=0, tiled=True)  167 us
    reduce_scatter x1, waiting for transfers between devices, on_device(): lax.psum_scatter(down_grad, 'fsdp', scatter_dimension=0, tiled=True)  166 us
    reduce_scatter x1, waiting for transfers between devices, on_device(): lax.psum_scatter(qkv_grad, 'fsdp', scatter_dimension=0, tiled=True)  128 us
    all_gather x1, waiting for transfers between devices, on_device(): lax.all_gather(up_weight, 'fsdp', axis=0, tiled=True)  80.4 us
    all_gather x1, waiting for transfers between devices, on_device(): lax.all_gather(down_weight, 'fsdp', axis=0, tiled=True)  66.8 us
    psum x1, waiting for transfers between devices, on_device(): lax.psum(shares[0].astype(jnp.bfloat16), 'dp').astype(jnp.float32)  30.7 us
    dot_general x4, matrix products, inner_rows(): lax.dot_general(left, right, (((0,), (0,)), ((), ())), preferred_element_...  29.1 us
    unnamed x1, blocking collectives  25.9 us
  transfers between devices with their start and end apart: 9, of which 9 were waited for; matrix products, arithmetic and copies ran while one was open for 10% of the time, Pallas kernels for 0%

commit v1 on v0

--- a/solution.py
+++ b/solution.py
@@ -1,8 +1,11 @@
+import functools
 import math
 
 import jax
 import jax.numpy as jnp
 from jax import lax
+from jax.experimental import pallas as pl
+from jax.experimental.pallas import tpu as pltpu
 from jax.sharding import PartitionSpec as P
 
 D = 1024
@@ -166,7 +169,848 @@
     return (input_grad, qkv_grad, out_grad, gain_one_grad, bias_one_grad)
 
 
-def on_device(
+MESH_ID = pl.DeviceIdType.MESH
+
+
+def aligned(index, size):
+    return pl.ds(pl.multiple_of(index * size, size), size)
+
+
+def greet(dp_index, fsdp_index, fsdp_size):
+    barrier = pltpu.get_barrier_semaphore()
+    peers = [(dp_index ^ 1, fsdp_index), (dp_index ^ 2, fsdp_index), (dp_index ^ 3, fsdp_index)]
+    peers += [(dp_index, lax.rem(fsdp_index + k, fsdp_size)) for k in range(1, fsdp_size)]
+    for peer in peers:
+        pl.semaphore_signal(barrier, inc=1, device_id=peer, device_id_type=MESH_ID)
+    pl.semaphore_wait(barrier, len(peers))
+
+
+def send(src, dst, send_sem, recv_sem, device):
+    return pltpu.make_async_remote_copy(
+        src_ref=src,
+        dst_ref=dst,
+        send_sem=send_sem,
+        recv_sem=recv_sem,
+        device_id=device,
+        device_id_type=MESH_ID,
+    )
+
+
+def gelu_parts(u):
+    cumul = 0.5 * (1.0 + lax.erf(u * (1.0 / math.sqrt(2.0))))
+    density = jnp.exp(-0.5 * u * u) * (1.0 / math.sqrt(2.0 * math.pi))
+    return u * cumul, cumul + u * density
+
+
+def head_scores(q_head, keys, key_valid):
+    scores = outer_cols(q_head, keys) * (1.0 / math.sqrt(HEAD_DIM))
+    masked = jnp.where(key_valid, scores, -1e30)
+    expont = jnp.exp(masked - jnp.max(masked, axis=-1, keepdims=True))
+    return expont / jnp.sum(expont, axis=-1, keepdims=True)
+
+
+def vector_row(small, row, fsdp_size):
+    values = small[...].astype(jnp.float32)
+    return jnp.concatenate([values[16 * f + row : 16 * f + row + 1] for f in range(fsdp_size)], axis=1)
+
+
+def transposed(target, source, fsdp_size):
+    rows = target.shape[2]
+
+    def body(n, carry):
+        target[lax.rem(n, 2), lax.div(n, 2)] = jnp.transpose(source[:, aligned(n, rows)])
+        return carry
+
+    lax.fori_loop(0, fsdp_size, body, 0)
+
+
+def forward_kernel(fsdp_size, *refs):
+    pieces = 4
+    length, scenes = refs[:2]
+    shards = refs[2:6]
+    small = refs[6]
+    fulls = refs[7:11]
+    layer_out, small_out = refs[11:13]
+    saved_out = refs[13:20]
+    rest = refs[20:]
+    weights = rest[:4]
+    small_full, hidden, qkv, attn, resid, normed, active = rest[4:11]
+    saved = rest[11:16]
+    (own_sem, zs, zr, xs, xr, ys, yr, ds, dr, es, er, cs, cr, ss, sr, load_sem, save_sem) = rest[16:]
+    hidden_t, hidden_two_t, attn_t, active_t, slope = saved
+    column = fsdp_size // 2
+    low, wide = jnp.bfloat16, jnp.float32
+    d = lax.axis_index("dp")
+    f = lax.axis_index("fsdp")
+    core = lax.rem(f, 2)
+    place = lax.div(f, 2)
+    x_peer, y_peer, c_peer = (d ^ 1, f), (d ^ 2, f), (d, f ^ 1)
+    seq_len = scenes.shape[0]
+
+    def block(piece, place_from, quarter, half=None):
+        rows = shards[piece].shape[0]
+        span = shards[piece].shape[1] // 4
+        row_part = aligned(place_from * 2 + core, rows)
+        if half is None:
+            return fulls[piece].at[row_part, aligned(quarter, span)]
+        return fulls[piece].at[row_part, aligned(quarter * 2 + half, span // 2)]
+
+    pending = []
+
+    def go(copy):
+        copy.start()
+        pending.append(copy)
+
+    def to_partner(piece, view):
+        send(view, view, cs.at[piece], cr.at[piece], c_peer).start()
+
+    def source(k):
+        return lax.rem(place - k + column, column)
+
+    def arrived(view, send_sem, recv_sem, device):
+        send(view, view, send_sem, recv_sem, device).wait_recv()
+
+    def from_column(piece, k):
+        at = (piece, k - 1)
+        view = block(piece, source(k), d)
+        arrived(view, zs.at[at], zr.at[at], x_peer)
+        go(send(view, view, xs.at[at], xr.at[at], x_peer))
+        go(send(view, view, ys.at[at], yr.at[at], y_peer))
+        to_partner(piece, view)
+
+    def from_sides(piece, k):
+        at = (piece, k - 1)
+        view = block(piece, source(k), d ^ 1)
+        arrived(view, xs.at[at], xr.at[at], x_peer)
+        part = block(piece, source(k), d ^ 1, 0)
+        go(send(part, part, ds.at[at], dr.at[at], y_peer))
+        to_partner(piece, view)
+        view = block(piece, source(k), d ^ 2)
+        arrived(view, ys.at[at], yr.at[at], y_peer)
+        part = block(piece, source(k), d ^ 2, 1)
+        go(send(part, part, es.at[at], er.at[at], x_peer))
+        to_partner(piece, view)
+
+    def from_corner(piece, k):
+        at = (piece, k - 1)
+        for half, (a, b, peer) in enumerate(((ds, dr, y_peer), (es, er, x_peer))):
+            part = block(piece, source(k), d ^ 3, half)
+            arrived(part, a.at[at], b.at[at], peer)
+            to_partner(piece, part)
+
+    def load(piece, part):
+        rows = fulls[piece].shape[0] // 8
+        at = pl.ds(part * rows, rows)
+        return pltpu.make_async_copy(fulls[piece].at[at], weights[piece].at[at], load_sem.at[piece, part])
+
+    def from_partner(piece, k):
+        rows = shards[piece].shape[0]
+        view = fulls[piece].at[pl.ds(0, rows * column)]
+        send(view, view, cs.at[piece], cr.at[piece], c_peer).wait()
+        own = fulls[piece].at[aligned(f, rows)]
+        pltpu.make_async_copy(weights[piece].at[aligned(f, rows)], own, own_sem.at[1, piece]).wait()
+        for part in range(8):
+            load(piece, part).start()
+
+    every = range(1, column)
+    order = []
+    order += [(from_column, 0, k) for k in every]
+    order += [(from_sides, 0, k) for k in every]
+    order += [(from_column, 1, k) for k in every]
+    order += [(from_corner, 0, k) for k in every] + [(from_partner, 0, 0)]
+    for piece in (1, 2, 3):
+        for k in every:
+            if piece < 3:
+                order.append((from_column, piece + 1, k))
+            order.append((from_sides, piece, k))
+        order += [(from_corner, piece, k) for k in every] + [(from_partner, piece, 0)]
+    done = []
+
+    def pump(count=1):
+        for _ in range(count):
+            if len(done) < len(order):
+                action, piece, k = order[len(done)]
+                done.append(1)
+                action(piece, k)
+
+    def pump_to(entry):
+        while order.index(entry) >= len(done):
+            pump()
+
+    greet(d, f, fsdp_size)
+    small_rows = small.shape[0]
+    for k in range(1, fsdp_size):
+        go(
+            send(
+                small,
+                small_full.at[aligned(f, small_rows)],
+                ss.at[k - 1],
+                sr.at[k - 1],
+                (d, lax.rem(f + k, fsdp_size)),
+            )
+        )
+    pltpu.make_async_copy(small, small_full.at[aligned(f, small_rows)], own_sem.at[0, pieces]).start()
+    for piece in range(pieces):
+        rows = shards[piece].shape[0]
+        span = shards[piece].shape[1] // 4
+        for k in every:
+            go(
+                send(
+                    shards[piece].at[:, aligned(d, span)],
+                    block(piece, place, d),
+                    zs.at[piece, k - 1],
+                    zr.at[piece, k - 1],
+                    (d, lax.rem(place + k, column) * 2 + core),
+                )
+            )
+        own = aligned(f, rows)
+        send(shards[piece], fulls[piece].at[own], cs.at[piece], cr.at[piece], c_peer).start()
+        pltpu.make_async_copy(shards[piece], weights[piece].at[own], own_sem.at[0, piece]).start()
+    for piece in range(pieces):
+        own = aligned(f, shards[piece].shape[0])
+        pltpu.make_async_copy(shards[piece], weights[piece].at[own], own_sem.at[0, piece]).wait()
+        pltpu.make_async_copy(weights[piece].at[own], fulls[piece].at[own], own_sem.at[1, piece]).start()
+
+    inputs = scenes[...].astype(wide)
+    normed_one, _ = norm_rows(inputs)
+    for k in range(1, fsdp_size):
+        view = small_full.at[aligned(lax.rem(f - k + fsdp_size, fsdp_size), small_rows)]
+        arrived(view, ss.at[k - 1], sr.at[k - 1], c_peer)
+    pltpu.make_async_copy(small, small_full.at[aligned(f, small_rows)], own_sem.at[0, pieces]).wait()
+    gain, bias = vector_row(small_full, 0, fsdp_size), vector_row(small_full, 1, fsdp_size)
+    hidden[...] = (normed_one * gain + bias).astype(low)
+    small_out[...] = small_full[...]
+    pump(2)
+    transposed(hidden_t, hidden, fsdp_size)
+    saves = []
+
+    def save(index, ref):
+        copy = pltpu.make_async_copy(ref, saved_out[index], save_sem.at[index])
+        saves.append(copy)
+        return copy
+
+    pump_to((from_partner, 0, 0))
+    save(0, hidden_t).start()
+    for part in range(8):
+        load(0, part).wait()
+
+    def project(n, carry):
+        cols = aligned(n, 512)
+        qkv[:, cols] = jnp.dot(hidden[...], weights[0][:, cols], preferred_element_type=wide).astype(low)
+        return carry
+
+    tiles = qkv.shape[1] // 512
+    lax.fori_loop(0, tiles // 2, project, 0)
+    pump(2)
+    lax.fori_loop(tiles // 2, tiles, project, 0)
+    pump(2)
+    save(1, qkv).start()
+    key_valid = lax.broadcasted_iota(jnp.int32, (1, seq_len), 1) < length[0]
+    first_half = lax.broadcasted_iota(jnp.int32, (1, 128), 1) < HEAD_DIM
+    halves = (first_half.astype(wide).astype(low), 1 - first_half.astype(wide).astype(low))
+    pairs = D // 128
+
+    def attend(j, carry):
+        queries, keys, values = (qkv[:, aligned(j + i * pairs, 128)] for i in range(3))
+        found = []
+        for half in halves:
+            probs = head_scores(queries * half, keys, key_valid)
+            found.append(jnp.dot(probs.astype(low), values, preferred_element_type=wide))
+        attn[:, aligned(j, 128)] = jnp.where(first_half, found[0], found[1]).astype(low)
+        return carry
+
+    for j in range(0, pairs, 2):
+        lax.fori_loop(j, j + 2, attend, 0)
+        pump(2)
+    pump_to((from_partner, 1, 0))
+    transposed(attn_t, attn, fsdp_size)
+    save(2, attn_t).start()
+    for part in range(8):
+        load(1, part).wait()
+
+    def second(n, carry):
+        cols = aligned(n, 512)
+        resid[:, cols] = scenes[:, cols].astype(wide) + jnp.dot(
+            attn[...], weights[1][:, cols], preferred_element_type=wide
+        )
+        return carry
+
+    lax.fori_loop(0, D // 512, second, 0)
+    save(3, resid).start()
+    normed_two, _ = norm_rows(resid[...])
+    gain, bias = vector_row(small_full, 2, fsdp_size), vector_row(small_full, 3, fsdp_size)
+    normed[...] = (normed_two * gain + bias).astype(low)
+    transposed(hidden_two_t, normed, fsdp_size)
+    save(4, hidden_two_t).start()
+    pump_to((from_partner, 2, 0))
+    for part in range(8):
+        load(2, part).wait()
+
+    def expand(n, carry):
+        cols = aligned(n, 256)
+        hidden_pre = jnp.dot(normed[...], weights[2][:, cols], preferred_element_type=wide)
+        acts, grads = gelu_parts(hidden_pre)
+        active[:, cols] = acts.astype(low)
+        slope[:, cols] = grads.astype(low)
+        return carry
+
+    spans = active.shape[1] // 256
+    for n in range(0, spans, 4):
+        lax.fori_loop(n, n + 4, expand, 0)
+        pump(1)
+    save(5, slope).start()
+    transposed(active_t, active, fsdp_size)
+    save(6, active_t).start()
+    pump_to((from_partner, 3, 0))
+    row_valid = lax.broadcasted_iota(jnp.int32, (seq_len, 1), 0) < length[0]
+    for part in range(8):
+        load(3, part).wait()
+        rows = pl.ds(part * (active.shape[1] // 8), active.shape[1] // 8)
+        resid_part = jnp.dot(active[:, rows], weights[3][rows], preferred_element_type=wide)
+        if part == 0:
+            saves[3].wait()
+        resid[...] += resid_part
+    layer_out[...] = jnp.where(row_valid, resid[...], 0.0).astype(low)
+    for copy in pending:
+        copy.wait_send()
+    for n, copy in enumerate(saves):
+        if n != 3:
+            copy.wait()
+
+
+def gather_forward(fsdp_size, length, scenes, shards, small):
+    pieces = len(shards)
+    hops = fsdp_size // 2 - 1
+    column = fsdp_size // 2
+    seq_len = scenes.shape[0]
+    ff = shards[3].shape[0] * fsdp_size
+    hbm = pl.BlockSpec(memory_space=pltpu.HBM)
+    vmem = pl.BlockSpec(memory_space=pltpu.VMEM)
+    smem = pl.BlockSpec(memory_space=pltpu.SMEM)
+    dma = pltpu.SemaphoreType.DMA
+    low, wide = jnp.bfloat16, jnp.float32
+    shape = jax.ShapeDtypeStruct
+    saved = [
+        ((2, column, D // fsdp_size, seq_len), low),
+        ((seq_len, 3 * D), low),
+        ((2, column, D // fsdp_size, seq_len), low),
+        ((seq_len, D), wide),
+        ((2, column, D // fsdp_size, seq_len), low),
+        ((seq_len, ff), low),
+        ((2, column, ff // fsdp_size, seq_len), low),
+    ]
+    full_shapes = [(a.shape[0] * fsdp_size, a.shape[1]) for a in shards]
+    small_shape = (small.shape[0] * fsdp_size, small.shape[1])
+    return pl.pallas_call(
+        functools.partial(forward_kernel, fsdp_size),
+        out_shape=[shape(s, low) for s in full_shapes]
+        + [shape((seq_len, D), low), shape(small_shape, low)]
+        + [shape(*s) for s in saved],
+        in_specs=[smem, vmem] + [hbm] * (pieces + 1),
+        out_specs=[hbm] * pieces + [vmem, vmem] + [hbm] * len(saved),
+        scratch_shapes=[pltpu.VMEM(s, low) for s in full_shapes]
+        + [
+            pltpu.VMEM(small_shape, low),
+            pltpu.VMEM((seq_len, D), low),
+            pltpu.VMEM((seq_len, 3 * D), low),
+            pltpu.VMEM((seq_len, D), low),
+            pltpu.VMEM((seq_len, D), wide),
+            pltpu.VMEM((seq_len, D), low),
+            pltpu.VMEM((seq_len, ff), low),
+        ]
+        + [pltpu.VMEM(*saved[i]) for i in (0, 4, 2, 6, 5)]
+        + [dma((2, pieces + 1))]
+        + [dma((pieces, hops))] * 10
+        + [dma((pieces,))] * 2
+        + [dma((fsdp_size - 1,))] * 2
+        + [dma((pieces, 8)), dma((len(saved),))],
+        compiler_params=pltpu.CompilerParams(
+            collective_id=0, has_side_effects=True, vmem_limit_bytes=62 << 20
+        ),
+        name="gather_forward",
+    )(length, scenes, *shards, small)
+
+
+def chunk_list(shapes):
+    chunks = []
+    for piece, (rows, span) in enumerate(shapes):
+        part = span // 8
+        high = min(rows, 128)
+        width = 256 if part % 256 == 0 else 128
+        for row in range(0, rows, high):
+            for col in range(0, part, width):
+                chunks.append((piece, row, high, part, col, width))
+    return chunks
+
+
+def backward_kernel(fsdp_size, chunks, *refs):
+    pieces = 4
+    count = len(chunks)
+    column = fsdp_size // 2
+    low, wide = jnp.bfloat16, jnp.float32
+    length, scenes, cotangent, small_full = refs[:4]
+    saved_in = refs[4:11]
+    fulls = refs[11:15]
+    outs = refs[15:19]
+    input_grad, small_out = refs[19:21]
+    rest = refs[21:]
+    sum_b, one_b, two_b, zed_b, fin_b = (rest[i * count : (i + 1) * count] for i in range(5))
+    rest = rest[5 * count :]
+    (other_b, core_b, weight, hidden_t, qkv, attn_t, resid, hidden_two_t, slope, active_t) = rest[:10]
+    (grad_low, grad_pre, grad_hidden, grad_resid, grad_attn, small_g, small_a, small_b) = rest[10:18]
+    (cs, cr, os_, or_, ts, tr, zs, zr, fs, fr, gs, gr, out_sem, ss, sr, us, ur) = rest[18:35]
+    save_sem, load_sem, credit = rest[35:]
+    d = lax.axis_index("dp")
+    f = lax.axis_index("fsdp")
+    core = lax.rem(f, 2)
+    place = lax.div(f, 2)
+    bits = (lax.rem(d, 2), lax.div(d, 2))
+    peers = ((d ^ 1, f), (d ^ 2, f))
+    c_peer = (d, f ^ 1)
+    seq_len = scenes.shape[0]
+    slots_other, slots_core = other_b.shape[0], core_b.shape[0]
+    pending = []
+    core_sends = {}
+
+    def go(copy):
+        copy.start()
+        pending.append(copy)
+        return copy
+
+    def arrived(view, send_sem, recv_sem, device):
+        send(view, view, send_sem, recv_sem, device).wait_recv()
+
+    def slot_view(ref, slot, i):
+        _, _, high, _, _, width = chunks[i]
+        return ref.at[slot, :, pl.ds(0, column * high), pl.ds(0, width)]
+
+    def fetch(index, ref):
+        return pltpu.make_async_copy(saved_in[index], ref, save_sem.at[index])
+
+    def grams(i, left_t, right):
+        piece, row, high, part, col, width = chunks[i]
+        slot = i % slots_other
+        if i >= slots_other:
+            core_sends[i - slots_other].wait_send()
+        step = 2 if width == part and width == 128 else 1
+
+        def fill(half, target):
+            left = left_t[half, :, pl.ds(row, high), :].reshape(column * high, seq_len)
+
+            def body(n, carry):
+                start = pl.multiple_of(n * step * part + col, 128)
+                found = jnp.dot(
+                    left, right[:, pl.ds(start, step * width)], preferred_element_type=wide
+                ).astype(low)
+                for m in range(step):
+                    target[n * step + m] = found[:, m * width : (m + 1) * width]
+                return carry
+
+            lax.fori_loop(0, 8 // step, body, 0)
+
+        fill(1 - core, slot_view(other_b, slot, i))
+        if i >= slots_core:
+            pl.semaphore_wait(credit, 1)
+        fill(core, sum_b[i])
+        copy = send(
+            slot_view(other_b, slot, i),
+            slot_view(core_b, i % slots_core, i),
+            cs.at[i],
+            cr.at[i],
+            c_peer,
+        )
+        copy.start()
+        core_sends[i] = copy
+
+    def add_into(target, other):
+        rows = target.shape[0]
+        strip = 64
+
+        def body(n, carry):
+            at = aligned(n, strip)
+            target[at] = (target[at].astype(wide) + other[at].astype(wide)).astype(low)
+            return carry
+
+        lax.fori_loop(0, rows // strip, body, 0)
+
+    def far_quarter(half, b):
+        if half == 0:
+            return (1 - bits[0]) + 2 * b
+        return b + 2 * (1 - bits[1])
+
+    def near_quarter(half, b):
+        if half == 0:
+            return bits[0] + 2 * b
+        return b + 2 * bits[1]
+
+    def pair(i):
+        view = slot_view(core_b, i % slots_core, i)
+        arrived(view, cs.at[i], cr.at[i], c_peer)
+
+        def add(quarter, half):
+            add_into(sum_b[i].at[quarter * 2 + half], view.at[quarter * 2 + half])
+
+        for b in range(2):
+            for half in range(2):
+                add(far_quarter(half, b), half)
+            for half in range(2):
+                go(
+                    send(
+                        sum_b[i].at[far_quarter(half, b) * 2 + half],
+                        one_b[i].at[half, b],
+                        os_.at[i, half, b],
+                        or_.at[i, half, b],
+                        peers[half],
+                    )
+                )
+        for b in range(2):
+            for half in range(2):
+                add(near_quarter(half, b), half)
+        if i + slots_core < count:
+            pl.semaphore_signal(credit, inc=1, device_id=c_peer, device_id_type=MESH_ID)
+
+    def first(i):
+        for half in range(2):
+            for b in range(2):
+                arrived(one_b[i].at[half, b], os_.at[i, half, b], or_.at[i, half, b], peers[half])
+                add_into(sum_b[i].at[near_quarter(half, b) * 2 + half], one_b[i].at[half, b])
+            other = d ^ 2 if half == 0 else d ^ 1
+            go(
+                send(
+                    sum_b[i].at[other * 2 + half],
+                    two_b[i].at[half],
+                    ts.at[i, half],
+                    tr.at[i, half],
+                    peers[1 - half],
+                )
+            )
+
+    def second(i):
+        _, _, high, _, _, _ = chunks[i]
+        for half in range(2):
+            arrived(two_b[i].at[half], ts.at[i, half], tr.at[i, half], peers[1 - half])
+            mine = sum_b[i].at[d * 2 + half]
+            add_into(mine, two_b[i].at[half])
+            for k in range(1, column):
+                to = lax.rem(place + k, column)
+                go(
+                    send(
+                        mine.at[aligned(to, high)],
+                        zed_b[i].at[half, k - 1],
+                        zs.at[i, half, k - 1],
+                        zr.at[i, half, k - 1],
+                        (d, to * 2 + core),
+                    )
+                )
+
+    def result(i, quarter, half):
+        piece, row, high, part, col, width = chunks[i]
+        start = pl.multiple_of((quarter * 2 + half) * part + col, 128)
+        return outs[piece].at[pl.ds(row, high), pl.ds(start, width)]
+
+    def last(i):
+        _, _, high, _, _, _ = chunks[i]
+        for half in range(2):
+            for k in range(1, column):
+                at = (i, half, k - 1)
+                arrived(zed_b[i].at[half, k - 1], zs.at[at], zr.at[at], c_peer)
+            total = sum_b[i][d * 2 + half, aligned(place, high)].astype(wide)
+            for k in range(1, column):
+                total = total + zed_b[i][half, k - 1].astype(wide)
+            fin_b[i][half] = total.astype(low)
+        for half in range(2):
+            mine = result(i, d, half)
+            pltpu.make_async_copy(fin_b[i].at[half], mine, out_sem.at[i, half]).start()
+            for axis in range(2):
+                at = (i, half, axis)
+                go(send(fin_b[i].at[half], mine, fs.at[at], fr.at[at], peers[axis]))
+
+    def spread(i):
+        for half in range(2):
+            for axis in range(2):
+                at = (i, half, axis)
+                view = result(i, d ^ (1 + axis), half)
+                arrived(view, fs.at[at], fr.at[at], peers[axis])
+                if half == axis:
+                    go(send(view, view, gs.at[i, half], gr.at[i, half], peers[1 - axis]))
+
+    def finish(i):
+        for half in range(2):
+            view = result(i, d ^ 3, half)
+            arrived(view, gs.at[i, half], gr.at[i, half], peers[1 - half])
+            pltpu.make_async_copy(fin_b[i].at[half], result(i, d, half), out_sem.at[i, half]).wait()
+
+    stages = (first, second, last, spread, finish)
+    order = []
+    for step in range(count + len(stages) - 1):
+        for n, stage in enumerate(stages):
+            if 0 <= step - n < count:
+                order.append((stage, step - n))
+    done = []
+    waiting = []
+    paired = []
+
+    def pair_up(keep=0):
+        while len(waiting) > keep:
+            i = waiting.pop(0)
+            pair(i)
+            paired.append(i)
+
+    def pump(limit=1):
+        pair_up()
+        for _ in range(limit):
+            if len(done) < len(order):
+                stage, i = order[len(done)]
+                if i not in paired:
+                    return
+                done.append(1)
+                stage(i)
+
+    def produce(piece, left_t, right, limit):
+        for i in range(count):
+            if chunks[i][0] == piece:
+                grams(i, left_t, right)
+                waiting.append(i)
+                pair_up(1)
+                for _ in range(limit):
+                    if len(done) < len(order) and order[len(done)][1] in paired:
+                        stage, n = order[len(done)]
+                        done.append(1)
+                        stage(n)
+
+    greet(d, f, fsdp_size)
+    big = weight
+    ff = fulls[3].shape[0]
+
+    def down_load(part):
+        rows = ff // 8
+        at = pl.ds(part * rows, rows)
+        return pltpu.make_async_copy(fulls[3].at[at], big.at[at], load_sem.at[3, part])
+
+    def up_load(part):
+        return pltpu.make_async_copy(
+            fulls[2].at[:, pl.ds(part * D, D)], big.at[pl.ds(part * D, D)], load_sem.at[2, part]
+        )
+
+    def qkv_load(part):
+        return pltpu.make_async_copy(
+            fulls[0].at[:, pl.ds(part * D, D)], big.at[pl.ds(part * D, D)], load_sem.at[0, part]
+        )
+
+    def out_load():
+        return pltpu.make_async_copy(fulls[1], big.at[pl.ds(3 * D, D)], load_sem.at[1, 0])
+
+    index = {"hidden_t": 0, "qkv": 1, "attn_t": 2, "resid": 3, "hidden_two_t": 4, "slope": 5, "active_t": 6}
+    held = dict(
+        hidden_t=hidden_t, qkv=qkv, attn_t=attn_t, resid=resid, hidden_two_t=hidden_two_t,
+        slope=slope, active_t=active_t,
+    )
+    for name in ("active_t", "slope"):
+        fetch(index[name], held[name]).start()
+    for part in range(8):
+        down_load(part).start()
+    for name in ("hidden_two_t", "resid", "attn_t", "qkv", "hidden_t"):
+        fetch(index[name], held[name]).start()
+
+    def got(name):
+        fetch(index[name], held[name]).wait()
+
+    row_valid = lax.broadcasted_iota(jnp.int32, (seq_len, 1), 0) < length[0]
+    grad_low[...] = jnp.where(row_valid, cotangent[...].astype(wide), 0.0).astype(low)
+    got("active_t")
+    produce(0, active_t, grad_low, 0)
+    got("slope")
+    for part in range(8):
+        down_load(part).wait()
+    tile = 512
+
+    def pre(n, carry):
+        at = aligned(n, tile)
+        back = outer_cols(grad_low[...], big[at])
+        grad_pre[:, at] = (back * slope[:, at].astype(wide)).astype(low)
+        return carry
+
+    for n in range(0, ff // tile, 2):
+        lax.fori_loop(n, n + 2, pre, 0)
+        pump(1)
+    for part in range(ff // D):
+        up_load(part).start()
+    got("hidden_two_t")
+    produce(1, hidden_two_t, grad_pre, 2)
+    for part in range(ff // D):
+        up_load(part).wait()
+        back = outer_cols(grad_pre[:, pl.ds(part * D, D)], big[pl.ds(part * D, D)])
+        if part == 0:
+            grad_hidden[...] = back
+        else:
+            grad_hidden[...] += back
+        pump(1)
+    for part in range(3):
+        qkv_load(part).start()
+    out_load().start()
+    got("resid")
+    pump(1)
+
+    def norm_step(values, grads, gain, base, row, target):
+        normed, inverse = norm_rows(values)
+        for n, total in enumerate((grads * normed, grads)):
+            sums = jnp.sum(total, axis=0, keepdims=True)
+            rows = D // fsdp_size
+            for to in range(fsdp_size):
+                small_g[to, row + n : row + n + 1, :] = sums[:, to * rows : (to + 1) * rows]
+        target[...] = base + norm_back(grads * gain, normed, inverse)
+
+    small_g[...] = jnp.zeros_like(small_g)
+    gain = vector_row(small_full, 2, fsdp_size)
+    base = jnp.where(row_valid, cotangent[...].astype(wide), 0.0)
+    norm_step(resid[...], grad_hidden[...], gain, base, 2, grad_resid)
+    grad_low[...] = grad_resid[...].astype(low)
+    pump(1)
+    got("attn_t")
+    produce(2, attn_t, grad_low, 2)
+    out_load().wait()
+
+    def attn_in(n, carry):
+        at = aligned(n, 256)
+        grad_attn[:, at] = outer_cols(
+            grad_low[...], big[pl.ds(pl.multiple_of(3 * D + n * 256, 256), 256)]
+        ).astype(low)
+        return carry
+
+    lax.fori_loop(0, D // 256, attn_in, 0)
+    got("qkv")
+    key_valid = lax.broadcasted_iota(jnp.int32, (1, seq_len), 1) < length[0]
+    first_half = lax.broadcasted_iota(jnp.int32, (1, 128), 1) < HEAD_DIM
+    halves = (first_half.astype(wide).astype(low), 1 - first_half.astype(wide).astype(low))
+    pairs = D // 128
+    factor = 1.0 / math.sqrt(HEAD_DIM)
+
+    def attend(j, carry):
+        queries, keys, values = (qkv[:, aligned(j + i * pairs, 128)] for i in range(3))
+        grads = grad_attn[:, aligned(j, 128)]
+        found = []
+        for half in halves:
+            probs = head_scores(queries * half, keys, key_valid)
+            grad_probs = outer_cols(grads * half, values)
+            row_dot = jnp.sum(probs * grad_probs, axis=-1, keepdims=True)
+            scores = (probs * (grad_probs - row_dot)).astype(low)
+            found.append(
+                (
+                    jnp.dot(scores, keys, preferred_element_type=wide) * factor,
+                    inner_rows(scores, queries) * factor,
+                    inner_rows(probs.astype(low), grads),
+                )
+            )
+        for i in range(3):
+            grad_pre[:, aligned(j + i * pairs, 128)] = jnp.where(
+                first_half, found[0][i], found[1][i]
+            ).astype(low)
+        return carry
+
+    for j in range(0, pairs, 2):
+        lax.fori_loop(j, j + 2, attend, 0)
+        pump(1)
+    got("hidden_t")
+    produce(3, hidden_t, grad_pre, 2)
+    for part in range(3):
+        qkv_load(part).wait()
+    for part in range(3):
+        total = outer_cols(grad_pre[:, pl.ds(part * D, D)], big[pl.ds(part * D, D)])
+        if part == 0:
+            grad_hidden[...] = total
+        else:
+            grad_hidden[...] += total
+    gain = vector_row(small_full, 0, fsdp_size)
+    norm_step(scenes[...].astype(wide), grad_hidden[...], gain, grad_resid[...], 0, grad_resid)
+    input_grad[...] = grad_resid[...].astype(low)
+    for k in range(1, fsdp_size):
+        to = lax.rem(f + k, fsdp_size)
+        go(send(small_g.at[to], small_a.at[k - 1], ss.at[k - 1], sr.at[k - 1], (d, to)))
+    pump(2)
+    total = small_g[f]
+    for k in range(1, fsdp_size):
+        arrived(small_a.at[k - 1], ss.at[k - 1], sr.at[k - 1], c_peer)
+        total = total + small_a[k - 1]
+    small_b[d] = total
+    pump(2)
+    for k in range(1, 4):
+        go(send(small_b.at[d], small_b.at[d], us.at[k - 1], ur.at[k - 1], (d ^ k, f)))
+    pump(4)
+    for k in range(1, 4):
+        arrived(small_b.at[d ^ k], us.at[k - 1], ur.at[k - 1], c_peer)
+    small_out[...] = (small_b[0] + small_b[1]) + (small_b[2] + small_b[3])
+    pump(len(order))
+    for copy in pending:
+        copy.wait_send()
+    for i in range(max(0, count - slots_other), count):
+        core_sends[i].wait_send()
+
+
+def reduce_backward(fsdp_size, length, scenes, cotangent, small_full, saved, fulls):
+    column = fsdp_size // 2
+    seq_len = scenes.shape[0]
+    ff = fulls[3].shape[0]
+    low, wide = jnp.bfloat16, jnp.float32
+    by_need = (fulls[3], fulls[2], fulls[1], fulls[0])
+    chunks = chunk_list([(w.shape[0] // fsdp_size, w.shape[1]) for w in by_need])
+    count = len(chunks)
+    hbm = pl.BlockSpec(memory_space=pltpu.HBM)
+    vmem = pl.BlockSpec(memory_space=pltpu.VMEM)
+    smem = pl.BlockSpec(memory_space=pltpu.SMEM)
+    dma = pltpu.SemaphoreType.DMA
+    scratch = []
+    for kind in ("sum", "one", "two", "zed", "fin"):
+        for _, _, high, _, _, width in chunks:
+            scratch.append(
+                pltpu.VMEM(
+                    {
+                        "sum": (8, column * high, width),
+                        "one": (2, 2, column * high, width),
+                        "two": (2, column * high, width),
+                        "zed": (2, column - 1, high, width),
+                        "fin": (2, high, width),
+                    }[kind],
+                    low,
+                )
+            )
+    tall = max(c[2] for c in chunks) * column
+    broad = max(c[5] for c in chunks)
+    scratch += [
+        pltpu.VMEM((2, 8, tall, broad), low),
+        pltpu.VMEM((2, 8, tall, broad), low),
+        pltpu.VMEM((ff, D), low),
+    ]
+    scratch += [pltpu.VMEM(a.shape, a.dtype) for a in saved]
+    scratch += [
+        pltpu.VMEM((seq_len, D), low),
+        pltpu.VMEM((seq_len, ff), low),
+        pltpu.VMEM((seq_len, D), wide),
+        pltpu.VMEM((seq_len, D), wide),
+        pltpu.VMEM((seq_len, D), low),
+        pltpu.VMEM((fsdp_size, 8, D // fsdp_size), wide),
+        pltpu.VMEM((fsdp_size - 1, 8, D // fsdp_size), wide),
+        pltpu.VMEM((4, 8, D // fsdp_size), wide),
+    ]
+    scratch += [dma((count,))] * 2 + [dma((count, 2, 2))] * 2 + [dma((count, 2))] * 2
+    scratch += [dma((count, 2, column - 1))] * 2 + [dma((count, 2, 2))] * 2 + [dma((count, 2))] * 2
+    scratch += [dma((count, 2))] + [dma((fsdp_size - 1,))] * 2 + [dma((3,))] * 2
+    scratch += [dma((len(saved),)), dma((4, 8)), pltpu.SemaphoreType.REGULAR]
+    shape = jax.ShapeDtypeStruct
+    return pl.pallas_call(
+        functools.partial(backward_kernel, fsdp_size, chunks),
+        out_shape=[shape((w.shape[0] // fsdp_size, w.shape[1]), low) for w in by_need]
+        + [shape((seq_len, D), low), shape((8, D // fsdp_size), wide)],
+        in_specs=[smem, vmem, vmem, vmem] + [hbm] * (len(saved) + 4),
+        out_specs=[hbm] * 4 + [vmem, vmem],
+        scratch_shapes=scratch,
+        compiler_params=pltpu.CompilerParams(
+            collective_id=1, has_side_effects=True, vmem_limit_bytes=67043328
+        ),
+        name="reduce_backward",
+    )(length, scenes, cotangent, small_full, *saved, *fulls)
+
+
+def on_device_wide(
     scenes_in,
     scene_lengths,
     cotangent,
@@ -256,6 +1100,55 @@
     )
 
 
+def on_device(
+    scenes_in,
+    scene_lengths,
+    cotangent,
+    qkv_weight,
+    out_weight,
+    up_weight,
+    down_weight,
+    gain_one,
+    bias_one,
+    gain_two,
+    bias_two,
+):
+    rows = gain_one.shape[0]
+    fsdp_size = D // rows
+    small = jnp.stack([gain_one, bias_one, gain_two, bias_two])
+    small = jnp.pad(small, ((0, 12), (0, 0)))
+    results = gather_forward(
+        fsdp_size,
+        scene_lengths,
+        scenes_in[0],
+        (qkv_weight, out_weight, up_weight, down_weight),
+        small,
+    )
+    fulls, layer_out, small_full, saved = results[:4], results[4], results[5], results[6:]
+    down_sum, up_sum, out_sum, qkv_sum, input_grad, small_sum = reduce_backward(
+        fsdp_size,
+        scene_lengths,
+        scenes_in[0],
+        cotangent[0],
+        small_full,
+        saved,
+        fulls,
+    )
+    wide = jnp.float32
+    return (
+        layer_out[None],
+        input_grad[None],
+        qkv_sum.astype(wide),
+        out_sum.astype(wide),
+        up_sum.astype(wide),
+        down_sum.astype(wide),
+        small_sum[0],
+        small_sum[1],
+        small_sum[2],
+        small_sum[3],
+    )
+
+
 def solution(mesh):
     placed = (
         P(("dp", "fsdp"), None, None),
@@ -270,8 +1163,9 @@
         P("fsdp"),
         P("fsdp"),
     )
+    body = on_device if mesh.shape["dp"] == 4 and mesh.shape["fsdp"] == 8 else on_device_wide
     return jax.shard_map(
-        on_device,
+        body,
         mesh=mesh,
         in_specs=placed,
         out_specs=(

time: 906 us -> 308 us (0.34)
  waiting for transfers between devices: 687 us -> 0 us
  Pallas kernels: 0 us -> 295 us
  matrix products: 85.6 us -> 0 us
  blocking collectives: 79.8 us -> 0 us
  other arithmetic: 27.9 us -> 8.62 us
  between operations: 15.4 us -> 1.32 us
    reduce_scatter x4 -> x0, waiting for transfers between devices: 469 us -> none  [the longest x1 167 us: on_device(): lax.psum_scatter(up_grad, 'fsdp', scatter_dimension=0, tiled=True)]
    pallas_call x0 -> x2, Pallas kernels: none -> 295 us  [the longest x1 164 us: reduce_backward(): pl.pallas_call(functools.partial(backward_kernel, fsdp_size, chunks), out...]
    all_gather x4 -> x0, waiting for transfers between devices: 184 us -> none  [the longest x1 80.4 us: on_device(): lax.all_gather(up_weight, 'fsdp', axis=0, tiled=True)]
    dot_general x18 -> x0, matrix products: 85.6 us -> none  [the longest x4 29.1 us: inner_rows(): lax.dot_general(left, right, (((0,), (0,)), ((), ())), preferred_element_...]
    all_gather x4 -> x0, blocking collectives: 43.6 us -> none  [the longest x1 13.6 us: on_device(): lax.all_gather(gain_one, 'fsdp', axis=0, tiled=True)]
    psum x1 -> x0, waiting for transfers between devices: 30.7 us -> none  [on_device(): lax.psum(shares[0].astype(jnp.bfloat16), 'dp').astype(jnp.float32)]
    unnamed x1 -> x0, blocking collectives: 25.9 us -> none
    convert_element_type x19 -> x4, other arithmetic: 20.5 us -> 7.31 us  [the longest x1 2.43 us: on_device(): qkv_sum.astype(wide)]
  transfers between devices with their start and end apart: 9 -> 0, of which waited for: 9 -> 0; matrix products, arithmetic and copies ran while one was open for 10% -> 0% of each run, Pallas kernels for 0% -> 0%
where the time goes in v1:
time: 308 us
  Pallas kernels  295 us (96%)
  other arithmetic  8.62 us (3%)
    pallas_call x1, Pallas kernels, reduce_backward(): pl.pallas_call(functools.partial(backward_kernel, fsdp_size, chunks), out...  164 us
    pallas_call x1, Pallas kernels, gather_forward(): pl.pallas_call(functools.partial(forward_kernel, fsdp_size), out_shape=[s...  131 us

profile of v1, /device:TPU:0, one launch (start us, length us, event | category | flops | bytes accessed | tf_op | source)
XLA Modules:
  0.0 307.6 jit_solution(6692113492172057194)
XLA Ops:
  1.3 1.3 fusion.6.refs_6_
  2.6 130.9 %gather_forward.1 = (bf16[1024,3072]{1,0:T(8,128)(2,1)}, bf16[1024,1024]{1,0:T(8,128)(2,1)}, bf16[1024,4096]{1,0:T(8,128)(2,1)}, bf16[4096,1024]{1,0:T(8,128)(2,...) custom-call(s32[1]{0:T(128)S(6)} %copy.23.refs_0_, ...), custom_call_target="tpu_custom_call" | custom-call | tf_op jit(solution)/shard_map/gather_forward/pallas_call | solution.py:504
  133.5 163.8 %reduce_backward.1 = (bf16[512,1024]{1,0:T(8,128)(2,1)}, bf16[128,4096]{1,0:T(8,128)(2,1)}, bf16[128,1024]{1,0:T(8,128)(2,1)}, bf16[128,3072]{1,0:T(8,128)(2,1)}...) custom-call(s32[1]{0:T(128)S(6)} %copy.23.refs_0_, bf16[256,1024]{1,0:T(8,128)(2,1)} %bitcast.17, ...), custom_call_target="tpu_custom_call" | custom-call | tf_op jit(solution)/shard_map/reduce_backward/pallas_call | solution.py:999
  297.3 0.0 copy-start.1
  297.3 1.4 slice_bitcast_fusion
  298.6 1.8 convert_element_type.15
  300.4 2.4 convert_element_type.14
  302.9 0.0 copy-done.1
  302.9 0.0 copy-start
  302.9 1.5 convert_element_type.16
  304.4 0.0 copy-done
  304.4 0.0 copy-start.2
  304.4 0.0 copy-start.3
  304.4 1.6 convert_element_type.17
  306.0 0.0 copy-done.2
  306.0 0.8 copy.24
  306.8 0.0 copy-done.3
  306.8 0.8 copy.25
Async XLA Ops:
  297.3 5.6 %copy-start.1 = (bf16[128,4096]{1,0:T(8,128)(2,1)S(1)}, bf16[128,4096]{1,0:T(8,128)(2,1)}, u32[]{:S(2)}) copy-start(bf16[128,4096]{1,0:T(8,128)(2,1)} %get-tuple-element.45) | copy-start | bytes 3145732
  302.9 1.5 copy-start
  304.4 1.6 copy-start.2
  304.4 2.4 copy-start.3

commit v2 on v0

--- a/solution.py
+++ b/solution.py
@@ -1,8 +1,11 @@
+import functools
 import math
 
 import jax
 import jax.numpy as jnp
 from jax import lax
+from jax.experimental import pallas as pl
+from jax.experimental.pallas import tpu as pltpu
 from jax.sharding import PartitionSpec as P
 
 D = 1024
@@ -166,7 +169,736 @@
     return (input_grad, qkv_grad, out_grad, gain_one_grad, bias_one_grad)
 
 
-def on_device(
+MESH_ID = pl.DeviceIdType.MESH
+
+
+def aligned(index, size):
+    return pl.ds(pl.multiple_of(index * size, size), size)
+
+
+def greet(dp_index, fsdp_index, fsdp_size):
+    barrier = pltpu.get_barrier_semaphore()
+    peers = [(dp_index ^ 1, fsdp_index), (dp_index ^ 2, fsdp_index), (dp_index ^ 3, fsdp_index)]
+    peers += [(dp_index, lax.rem(fsdp_index + k, fsdp_size)) for k in range(1, fsdp_size)]
+    for peer in peers:
+        pl.semaphore_signal(barrier, inc=1, device_id=peer, device_id_type=MESH_ID)
+    pl.semaphore_wait(barrier, len(peers))
+
+
+def send(src, dst, send_sem, recv_sem, device):
+    return pltpu.make_async_remote_copy(
+        src_ref=src,
+        dst_ref=dst,
+        send_sem=send_sem,
+        recv_sem=recv_sem,
+        device_id=device,
+        device_id_type=MESH_ID,
+    )
+
+
+def gelu_parts(u):
+    cumul = 0.5 * (1.0 + lax.erf(u * (1.0 / math.sqrt(2.0))))
+    density = jnp.exp(-0.5 * u * u) * (1.0 / math.sqrt(2.0 * math.pi))
+    return u * cumul, cumul + u * density
+
+
+def head_scores(q_head, keys, key_valid):
+    scores = outer_cols(q_head, keys) * (1.0 / math.sqrt(HEAD_DIM))
+    masked = jnp.where(key_valid, scores, -1e30)
+    expont = jnp.exp(masked - jnp.max(masked, axis=-1, keepdims=True))
+    return expont / jnp.sum(expont, axis=-1, keepdims=True)
+
+
+def transposed(target, source, fsdp_size):
+    rows = target.shape[2]
+
+    def body(n, carry):
+        target[lax.rem(n, 2), lax.div(n, 2)] = jnp.transpose(source[:, aligned(n, rows)])
+        return carry
+
+    lax.fori_loop(0, fsdp_size, body, 0)
+
+
+SLOTS = 2
+
+
+def chunk_list(shapes):
+    chunks = []
+    for piece, (rows, span) in enumerate(shapes):
+        part = span // 8
+        high = min(rows, 128)
+        width = 256 if part % 256 == 0 else 128
+        for row in range(0, rows, high):
+            for col in range(0, part, width):
+                chunks.append((piece, row, high, part, col, width))
+    return chunks
+
+
+def layer_kernel(fsdp_size, chunks, *refs):
+    pieces = 4
+    count = len(chunks)
+    column = fsdp_size // 2
+    low, wide = jnp.bfloat16, jnp.float32
+    length, scenes, cotangent = refs[:3]
+    shards = refs[3:7]
+    small = refs[7]
+    fulls = refs[8:12]
+    outs = refs[12:16]
+    layer_out, input_grad, small_out = refs[16:19]
+    rest = refs[19:]
+    sum_b, one_b, two_b, zed_b, fin_b = (rest[i * count : (i + 1) * count] for i in range(5))
+    rest = rest[5 * count :]
+    other_b, core_b, big, small_full, hidden, hidden_t, qkv, attn, attn_t = rest[:9]
+    resid, hidden_two_t, wide_low, slope, active_t, grad_low, grad_hidden, grad_resid = rest[9:17]
+    small_g, small_a, small_b = rest[17:20]
+    own_sem, az, bz, ax, bx, ay, by, ad, bd, ae, be, ac, bc, sv, rv = rest[20:35]
+    (cs, cr, os_, or_, ts, tr, zs, zr, fs, fr, gs, gr, out_sem, ss, sr, us, ur) = rest[35:52]
+    load_sem, credit = rest[52:]
+    d = lax.axis_index("dp")
+    f = lax.axis_index("fsdp")
+    core = lax.rem(f, 2)
+    place = lax.div(f, 2)
+    bits = (lax.rem(d, 2), lax.div(d, 2))
+    x_peer, y_peer, c_peer = (d ^ 1, f), (d ^ 2, f), (d, f ^ 1)
+    peers = (x_peer, y_peer)
+    seq_len = scenes.shape[0]
+    ff = wide_low.shape[1]
+    slots_other, slots_core = other_b.shape[0], core_b.shape[0]
+    pending = []
+    core_sends = {}
+
+    def go(copy):
+        copy.start()
+        pending.append(copy)
+
+    def arrived(view, send_sem, recv_sem, device):
+        send(view, view, send_sem, recv_sem, device).wait_recv()
+
+    def block(piece, place_from, quarter, half=None):
+        rows = shards[piece].shape[0]
+        span = shards[piece].shape[1] // 4
+        row_part = aligned(place_from * 2 + core, rows)
+        if half is None:
+            return fulls[piece].at[row_part, aligned(quarter, span)]
+        return fulls[piece].at[row_part, aligned(quarter * 2 + half, span // 2)]
+
+    def to_partner(piece, view):
+        send(view, view, ac.at[piece], bc.at[piece], c_peer).start()
+
+    def source(k):
+        return lax.rem(place - k + column, column)
+
+    def from_column(piece, k):
+        at = (piece, k - 1)
+        view = block(piece, source(k), d)
+        arrived(view, az.at[at], bz.at[at], x_peer)
+        go(send(view, view, ax.at[at], bx.at[at], x_peer))
+        go(send(view, view, ay.at[at], by.at[at], y_peer))
+        to_partner(piece, view)
+
+    def from_sides(piece, k):
+        at = (piece, k - 1)
+        view = block(piece, source(k), d ^ 1)
+        arrived(view, ax.at[at], bx.at[at], x_peer)
+        part = block(piece, source(k), d ^ 1, 0)
+        go(send(part, part, ad.at[at], bd.at[at], y_peer))
+        to_partner(piece, view)
+        view = block(piece, source(k), d ^ 2)
+        arrived(view, ay.at[at], by.at[at], y_peer)
+        part = block(piece, source(k), d ^ 2, 1)
+        go(send(part, part, ae.at[at], be.at[at], x_peer))
+        to_partner(piece, view)
+
+    def from_corner(piece, k):
+        at = (piece, k - 1)
+        for half, (a, b, peer) in enumerate(((ad, bd, y_peer), (ae, be, x_peer))):
+            part = block(piece, source(k), d ^ 3, half)
+            arrived(part, a.at[at], b.at[at], peer)
+            to_partner(piece, part)
+
+    def from_partner(piece):
+        rows = shards[piece].shape[0]
+        view = fulls[piece].at[pl.ds(0, rows * column)]
+        send(view, view, ac.at[piece], bc.at[piece], c_peer).wait()
+
+    def loads(piece):
+        if piece == 3:
+            parts = [(fulls[3].at[pl.ds(n * D, D)], pl.ds(n * D, D)) for n in range(ff // D)]
+        elif piece == 1:
+            parts = [(fulls[1], pl.ds(3 * D, D))]
+        else:
+            parts = [
+                (fulls[piece].at[:, pl.ds(n * D, D)], pl.ds(n * D, D))
+                for n in range(fulls[piece].shape[1] // D)
+            ]
+        return [
+            pltpu.make_async_copy(view, big.at[at], load_sem.at[piece, n])
+            for n, (view, at) in enumerate(parts)
+        ]
+
+    def own_parts(piece, back):
+        rows, span = shards[piece].shape
+        first_row = sum(s.shape[0] * (s.shape[1] // D) for s in shards[:piece])
+        parts = []
+        for n in range(span // D):
+            stage = big.at[pl.ds(first_row + n * rows, rows)]
+            cols = pl.ds(n * D, D)
+            whole = fulls[piece].at[aligned(f, rows), cols]
+            ends = (stage, whole) if back else (shards[piece].at[:, cols], stage)
+            parts.append(pltpu.make_async_copy(*ends, own_sem.at[int(back), piece, n]))
+        return parts
+
+    every = range(1, column)
+    blocks = [(piece, k) for piece in range(pieces) for k in every]
+    gather_order = []
+    for n in range(len(blocks) + 4):
+        for action, lag in ((from_column, 0), (from_sides, 1), (from_corner, 2)):
+            if 0 <= n - lag < len(blocks):
+                gather_order.append((action, *blocks[n - lag]))
+    gathered = []
+
+    def gather_step(limit=1):
+        for _ in range(limit):
+            if len(gathered) < len(gather_order):
+                action, piece, k = gather_order[len(gathered)]
+                gathered.append(1)
+                action(piece, k)
+
+    def gather_to(action, piece):
+        last_one = gather_order.index((action, piece, column - 1))
+        while len(gathered) <= last_one:
+            gather_step()
+
+    def slot_view(ref, slot, i):
+        _, _, high, _, _, width = chunks[i]
+        return ref.at[slot, :, pl.ds(0, column * high), pl.ds(0, width)]
+
+    def grams(i, left_t, right):
+        piece, row, high, part, col, width = chunks[i]
+        slot = i % slots_other
+        if i >= slots_other:
+            core_sends[i - slots_other].wait_send()
+        step = 2 if width == part and width == 128 else 1
+
+        def fill(half, target):
+            left = left_t[half, :, pl.ds(row, high), :].reshape(column * high, seq_len)
+
+            def body(n, carry):
+                start = pl.multiple_of(n * step * part + col, 128)
+                found = jnp.dot(
+                    left, right[:, pl.ds(start, step * width)], preferred_element_type=wide
+                ).astype(low)
+                for m in range(step):
+                    target[n * step + m] = found[:, m * width : (m + 1) * width]
+                return carry
+
+            lax.fori_loop(0, 8 // step, body, 0)
+
+        fill(1 - core, slot_view(other_b, slot, i))
+        if i >= slots_core:
+            pl.semaphore_wait(credit, 1)
+        fill(core, sum_b[i])
+        copy = send(
+            slot_view(other_b, slot, i),
+            slot_view(core_b, i % slots_core, i),
+            cs.at[i],
+            cr.at[i],
+            c_peer,
+        )
+        copy.start()
+        core_sends[i] = copy
+
+    def add_into(target, other):
+        rows = target.shape[0]
+        strip = 64
+
+        def body(n, carry):
+            at = aligned(n, strip)
+            target[at] = (target[at].astype(wide) + other[at].astype(wide)).astype(low)
+            return carry
+
+        lax.fori_loop(0, rows // strip, body, 0)
+
+    def far_quarter(half, b):
+        if half == 0:
+            return (1 - bits[0]) + 2 * b
+        return b + 2 * (1 - bits[1])
+
+    def near_quarter(half, b):
+        if half == 0:
+            return bits[0] + 2 * b
+        return b + 2 * bits[1]
+
+    def pair(i):
+        view = slot_view(core_b, i % slots_core, i)
+        arrived(view, cs.at[i], cr.at[i], c_peer)
+
+        def add(quarter, half):
+            add_into(sum_b[i].at[quarter * 2 + half], view.at[quarter * 2 + half])
+
+        for b in range(2):
+            for half in range(2):
+                add(far_quarter(half, b), half)
+            for half in range(2):
+                go(
+                    send(
+                        sum_b[i].at[far_quarter(half, b) * 2 + half],
+                        one_b[i].at[half, b],
+                        os_.at[i, half, b],
+                        or_.at[i, half, b],
+                        peers[half],
+                    )
+                )
+        for b in range(2):
+            for half in range(2):
+                add(near_quarter(half, b), half)
+        if i + slots_core < count:
+            pl.semaphore_signal(credit, inc=1, device_id=c_peer, device_id_type=MESH_ID)
+
+    def first(i):
+        for half in range(2):
+            for b in range(2):
+                arrived(one_b[i].at[half, b], os_.at[i, half, b], or_.at[i, half, b], peers[half])
+                add_into(sum_b[i].at[near_quarter(half, b) * 2 + half], one_b[i].at[half, b])
+            other = d ^ 2 if half == 0 else d ^ 1
+            go(
+                send(
+                    sum_b[i].at[other * 2 + half],
+                    two_b[i].at[half],
+                    ts.at[i, half],
+                    tr.at[i, half],
+                    peers[1 - half],
+                )
+            )
+
+    def second(i):
+        _, _, high, _, _, _ = chunks[i]
+        for half in range(2):
+            arrived(two_b[i].at[half], ts.at[i, half], tr.at[i, half], peers[1 - half])
+            mine = sum_b[i].at[d * 2 + half]
+            add_into(mine, two_b[i].at[half])
+            for k in range(1, column):
+                to = lax.rem(place + k, column)
+                go(
+                    send(
+                        mine.at[aligned(to, high)],
+                        zed_b[i].at[half, k - 1],
+                        zs.at[i, half, k - 1],
+                        zr.at[i, half, k - 1],
+                        (d, to * 2 + core),
+                    )
+                )
+
+    def result(i, quarter, half):
+        piece, row, high, part, col, width = chunks[i]
+        start = pl.multiple_of((quarter * 2 + half) * part + col, 128)
+        return outs[piece].at[pl.ds(row, high), pl.ds(start, width)]
+
+    def last(i):
+        _, _, high, _, _, _ = chunks[i]
+        for half in range(2):
+            for k in range(1, column):
+                at = (i, half, k - 1)
+                arrived(zed_b[i].at[half, k - 1], zs.at[at], zr.at[at], c_peer)
+            total = sum_b[i][d * 2 + half, aligned(place, high)].astype(wide)
+            for k in range(1, column):
+                total = total + zed_b[i][half, k - 1].astype(wide)
+            fin_b[i][half] = total.astype(low)
+        for half in range(2):
+            mine = result(i, d, half)
+            pltpu.make_async_copy(fin_b[i].at[half], mine, out_sem.at[i, half]).start()
+            for axis in range(2):
+                at = (i, half, axis)
+                go(send(fin_b[i].at[half], mine, fs.at[at], fr.at[at], peers[axis]))
+
+    def spread(i):
+        for half in range(2):
+            for axis in range(2):
+                at = (i, half, axis)
+                view = result(i, d ^ (1 + axis), half)
+                arrived(view, fs.at[at], fr.at[at], peers[axis])
+                if half == axis:
+                    go(send(view, view, gs.at[i, half], gr.at[i, half], peers[1 - axis]))
+
+    def finish(i):
+        for half in range(2):
+            view = result(i, d ^ 3, half)
+            arrived(view, gs.at[i, half], gr.at[i, half], peers[1 - half])
+            pltpu.make_async_copy(fin_b[i].at[half], result(i, d, half), out_sem.at[i, half]).wait()
+
+    stages = (first, second, last, spread, finish)
+    order = []
+    for step in range(count + len(stages) - 1):
+        for n, stage in enumerate(stages):
+            if 0 <= step - n < count:
+                order.append((stage, step - n))
+    done = []
+    waiting = []
+    paired = []
+
+    def pair_up(keep=0):
+        while len(waiting) > keep:
+            i = waiting.pop(0)
+            pair(i)
+            paired.append(i)
+
+    def advance(limit):
+        for _ in range(limit):
+            if len(done) < len(order) and order[len(done)][1] in paired:
+                stage, i = order[len(done)]
+                done.append(1)
+                stage(i)
+
+    def pump(limit=1):
+        pair_up()
+        advance(limit)
+
+    def produce(some, left_t, right, limit, keep=1):
+        for i in some:
+            pair_up(slots_core - 1)
+            grams(i, left_t, right)
+            waiting.append(i)
+            pair_up(keep)
+            advance(limit)
+
+    by_piece = [[i for i in range(count) if chunks[i][0] == piece] for piece in range(pieces)]
+
+    greet(d, f, fsdp_size)
+    small_rows = small.shape[0]
+    for k in range(1, fsdp_size):
+        to = lax.rem(f + k, fsdp_size)
+        go(send(small, small_full.at[aligned(f, small_rows)], sv.at[k - 1], rv.at[k - 1], (d, to)))
+    own_small = pltpu.make_async_copy(
+        small, small_full.at[aligned(f, small_rows)], own_sem.at[0, 0, pieces]
+    )
+    own_small.start()
+    for piece in range(pieces):
+        rows, span = shards[piece].shape
+        for k in every:
+            go(
+                send(
+                    shards[piece].at[:, aligned(d, span // 4)],
+                    block(piece, place, d),
+                    az.at[piece, k - 1],
+                    bz.at[piece, k - 1],
+                    (d, lax.rem(place + k, column) * 2 + core),
+                )
+            )
+        own = fulls[piece].at[aligned(f, rows)]
+        send(shards[piece], own, ac.at[piece], bc.at[piece], c_peer).start()
+        for copy in own_parts(piece, False):
+            copy.start()
+    for piece in range(pieces):
+        for copy in own_parts(piece, False):
+            copy.wait()
+        for copy in own_parts(piece, True):
+            copy.start()
+
+    normed_one, _ = norm_rows(scenes[...].astype(wide))
+    for k in range(1, fsdp_size):
+        view = small_full.at[aligned(lax.rem(f - k + fsdp_size, fsdp_size), small_rows)]
+        arrived(view, sv.at[k - 1], rv.at[k - 1], c_peer)
+    own_small.wait()
+
+    def vector(row):
+        values = small_full[...].astype(wide)
+        at = range(row, small_rows * fsdp_size, small_rows)
+        return jnp.concatenate([values[n : n + 1] for n in at], axis=1)
+
+    hidden[...] = (normed_one * vector(0) + vector(1)).astype(low)
+    gather_step(2)
+    transposed(hidden_t, hidden, fsdp_size)
+    for piece in range(pieces):
+        for copy in own_parts(piece, True):
+            copy.wait()
+    gather_to(from_corner, 0)
+    gather_step(3)
+    from_partner(0)
+    for copy in loads(0):
+        copy.start()
+    gather_step(1)
+    for copy in loads(0):
+        copy.wait()
+
+    def project(n, carry):
+        cols = aligned(n, 512)
+        rows = aligned(lax.div(n, D // 512), D)
+        weight = big[rows, aligned(lax.rem(n, D // 512), 512)]
+        qkv[:, cols] = jnp.dot(hidden[...], weight, preferred_element_type=wide).astype(low)
+        return carry
+
+    tiles = qkv.shape[1] // 512
+    lax.fori_loop(0, tiles // 2, project, 0)
+    gather_step(2)
+    lax.fori_loop(tiles // 2, tiles, project, 0)
+    gather_step(2)
+    key_valid = lax.broadcasted_iota(jnp.int32, (1, seq_len), 1) < length[0]
+    row_valid = lax.broadcasted_iota(jnp.int32, (seq_len, 1), 0) < length[0]
+    first_half = lax.broadcasted_iota(jnp.int32, (1, 128), 1) < HEAD_DIM
+    halves = (first_half.astype(wide).astype(low), 1 - first_half.astype(wide).astype(low))
+    pairs = D // 128
+
+    def attend(j, carry):
+        queries, keys, values = (qkv[:, aligned(j + i * pairs, 128)] for i in range(3))
+        found = []
+        for half in halves:
+            probs = head_scores(queries * half, keys, key_valid)
+            found.append(jnp.dot(probs.astype(low), values, preferred_element_type=wide))
+        attn[:, aligned(j, 128)] = jnp.where(first_half, found[0], found[1]).astype(low)
+        return carry
+
+    for j in range(0, pairs, 2):
+        lax.fori_loop(j, j + 2, attend, 0)
+        gather_step(2)
+    transposed(attn_t, attn, fsdp_size)
+    gather_to(from_corner, 1)
+    gather_step(1)
+    from_partner(1)
+    for copy in loads(1):
+        copy.start()
+    for copy in loads(1):
+        copy.wait()
+
+    def second_in(n, carry):
+        cols = aligned(n, 512)
+        resid[:, cols] = scenes[:, cols].astype(wide) + jnp.dot(
+            attn[...], big[pl.ds(3 * D, D), cols], preferred_element_type=wide
+        )
+        return carry
+
+    lax.fori_loop(0, D // 512, second_in, 0)
+    normed_two, _ = norm_rows(resid[...])
+    hidden[...] = (normed_two * vector(2) + vector(3)).astype(low)
+    transposed(hidden_two_t, hidden, fsdp_size)
+    gather_to(from_corner, 2)
+    gather_step(2)
+    from_partner(2)
+    for copy in loads(2):
+        copy.start()
+    span = D // 256
+
+    def expand(n, carry):
+        cols = aligned(n, 256)
+        rows = aligned(lax.div(n, span), D)
+        weight = big[rows, aligned(lax.rem(n, span), 256)]
+        acts, grads = gelu_parts(jnp.dot(hidden[...], weight, preferred_element_type=wide))
+        wide_low[:, cols] = acts.astype(low)
+        slope[:, cols] = grads.astype(low)
+        return carry
+
+    for part, copy in enumerate(loads(2)):
+        copy.wait()
+        lax.fori_loop(part * span, (part + 1) * span, expand, 0)
+        gather_step(2)
+    transposed(active_t, wide_low, fsdp_size)
+    grad_low[...] = jnp.where(row_valid, cotangent[...].astype(wide), 0.0).astype(low)
+    early = by_piece[0][: slots_core - 1]
+    produce(early, active_t, grad_low, 0, slots_core)
+    gather_to(from_sides, pieces - 1)
+    pair_up()
+    gather_to(from_corner, pieces - 1)
+    produce(by_piece[0][len(early) :][:1], active_t, grad_low, 0)
+    from_partner(3)
+    for copy in loads(3):
+        copy.start()
+    produce(by_piece[0][len(early) + 1 :], active_t, grad_low, 0)
+    for part, copy in enumerate(loads(3)):
+        copy.wait()
+        at = pl.ds(part * D, D)
+        term = jnp.dot(wide_low[:, at], big[at], preferred_element_type=wide)
+        if part == 0:
+            grad_hidden[...] = resid[...] + term
+        else:
+            grad_hidden[...] += term
+        pair_up()
+    layer_out[...] = jnp.where(row_valid, grad_hidden[...], 0.0).astype(low)
+    pump(1)
+
+    tile = 512
+
+    def pre(n, carry):
+        at = aligned(n, tile)
+        back = outer_cols(grad_low[...], big[at])
+        wide_low[:, at] = (back * slope[:, at].astype(wide)).astype(low)
+        return carry
+
+    for n in range(0, ff // tile, 2):
+        lax.fori_loop(n, n + 2, pre, 0)
+        pump(1)
+    for copy in loads(2):
+        copy.start()
+    produce(by_piece[1], hidden_two_t, wide_low, 2)
+    for part, copy in enumerate(loads(2)):
+        copy.wait()
+        back = outer_cols(wide_low[:, pl.ds(part * D, D)], big[pl.ds(part * D, D)])
+        if part == 0:
+            grad_hidden[...] = back
+        else:
+            grad_hidden[...] += back
+        pump(1)
+    for piece in (1, 0):
+        for copy in loads(piece):
+            copy.start()
+    pump(1)
+
+    def norm_step(values, grads, gain, base, row):
+        normed, inverse = norm_rows(values)
+        rows = D // fsdp_size
+        for n, total in enumerate((grads * normed, grads)):
+            sums = jnp.sum(total, axis=0, keepdims=True)
+            for to in range(fsdp_size):
+                small_g[to, row + n : row + n + 1, :] = sums[:, to * rows : (to + 1) * rows]
+        return base + norm_back(grads * gain, normed, inverse)
+
+    small_g[...] = jnp.zeros_like(small_g)
+    base = jnp.where(row_valid, cotangent[...].astype(wide), 0.0)
+    grad_resid[...] = norm_step(resid[...], grad_hidden[...], vector(2), base, 2)
+    grad_low[...] = grad_resid[...].astype(low)
+    pump(1)
+    produce(by_piece[2], attn_t, grad_low, 2)
+    for copy in loads(1):
+        copy.wait()
+
+    def attn_in(n, carry):
+        rows = pl.ds(pl.multiple_of(3 * D + n * 256, 256), 256)
+        attn[:, aligned(n, 256)] = outer_cols(grad_low[...], big[rows]).astype(low)
+        return carry
+
+    lax.fori_loop(0, D // 256, attn_in, 0)
+    pump(1)
+    factor = 1.0 / math.sqrt(HEAD_DIM)
+
+    def attend_back(j, carry):
+        queries, keys, values = (qkv[:, aligned(j + i * pairs, 128)] for i in range(3))
+        grads = attn[:, aligned(j, 128)]
+        found = []
+        for half in halves:
+            probs = head_scores(queries * half, keys, key_valid)
+            grad_probs = outer_cols(grads * half, values)
+            row_dot = jnp.sum(probs * grad_probs, axis=-1, keepdims=True)
+            scores = (probs * (grad_probs - row_dot)).astype(low)
+            found.append(
+                (
+                    jnp.dot(scores, keys, preferred_element_type=wide) * factor,
+                    inner_rows(scores, queries) * factor,
+                    inner_rows(probs.astype(low), grads),
+                )
+            )
+        for i in range(3):
+            wide_low[:, aligned(j + i * pairs, 128)] = jnp.where(
+                first_half, found[0][i], found[1][i]
+            ).astype(low)
+        return carry
+
+    for j in range(0, pairs, 2):
+        lax.fori_loop(j, j + 2, attend_back, 0)
+        pump(1)
+    produce(by_piece[3], hidden_t, wide_low, 2)
+    for part, copy in enumerate(loads(0)):
+        copy.wait()
+        total = outer_cols(wide_low[:, pl.ds(part * D, D)], big[pl.ds(part * D, D)])
+        if part == 0:
+            grad_hidden[...] = total
+        else:
+            grad_hidden[...] += total
+    pump(1)
+    total = norm_step(scenes[...].astype(wide), grad_hidden[...], vector(0), grad_resid[...], 0)
+    input_grad[...] = total.astype(low)
+    for k in range(1, fsdp_size):
+        to = lax.rem(f + k, fsdp_size)
+        go(send(small_g.at[to], small_a.at[k - 1], ss.at[k - 1], sr.at[k - 1], (d, to)))
+    pump(2)
+    total = small_g[f]
+    for k in range(1, fsdp_size):
+        arrived(small_a.at[k - 1], ss.at[k - 1], sr.at[k - 1], c_peer)
+        total = total + small_a[k - 1]
+    small_b[d] = total
+    pump(2)
+    for k in range(1, 4):
+        go(send(small_b.at[d], small_b.at[d], us.at[k - 1], ur.at[k - 1], (d ^ k, f)))
+    pump(4)
+    for k in range(1, 4):
+        arrived(small_b.at[d ^ k], us.at[k - 1], ur.at[k - 1], c_peer)
+    small_out[...] = (small_b[0] + small_b[1]) + (small_b[2] + small_b[3])
+    pump(len(order))
+    for copy in pending:
+        copy.wait_send()
+    for i in range(max(0, count - slots_other), count):
+        core_sends[i].wait_send()
+
+
+def layer_step(fsdp_size, length, scenes, cotangent, shards, small):
+    column = fsdp_size // 2
+    hops = column - 1
+    seq_len = scenes.shape[0]
+    ff = shards[3].shape[0] * fsdp_size
+    low, wide = jnp.bfloat16, jnp.float32
+    by_need = (shards[3], shards[2], shards[1], shards[0])
+    chunks = chunk_list([w.shape for w in by_need])
+    count = len(chunks)
+    hbm = pl.BlockSpec(memory_space=pltpu.HBM)
+    vmem = pl.BlockSpec(memory_space=pltpu.VMEM)
+    smem = pl.BlockSpec(memory_space=pltpu.SMEM)
+    dma = pltpu.SemaphoreType.DMA
+    shape = jax.ShapeDtypeStruct
+    scratch = []
+    for kind in ("sum", "one", "two", "zed", "fin"):
+        for _, _, high, _, _, width in chunks:
+            buffers = {
+                "sum": (8, column * high, width),
+                "one": (2, 2, column * high, width),
+                "two": (2, column * high, width),
+                "zed": (2, hops, high, width),
+                "fin": (2, high, width),
+            }
+            scratch.append(pltpu.VMEM(buffers[kind], low))
+    tall = max(c[2] for c in chunks) * column
+    broad = max(c[5] for c in chunks)
+    rows = D // fsdp_size
+    turned = pltpu.VMEM((2, column, rows, seq_len), low)
+    scratch += [pltpu.VMEM((SLOTS, 8, tall, broad), low)] * 2
+    scratch += [
+        pltpu.VMEM((ff, D), low),
+        pltpu.VMEM((small.shape[0] * fsdp_size, small.shape[1]), low),
+        pltpu.VMEM((seq_len, D), low),
+        turned,
+        pltpu.VMEM((seq_len, 3 * D), low),
+        pltpu.VMEM((seq_len, D), low),
+        turned,
+        pltpu.VMEM((seq_len, D), wide),
+        turned,
+        pltpu.VMEM((seq_len, ff), low),
+        pltpu.VMEM((seq_len, ff), low),
+        pltpu.VMEM((2, column, ff // fsdp_size, seq_len), low),
+        pltpu.VMEM((seq_len, D), low),
+        pltpu.VMEM((seq_len, D), wide),
+        pltpu.VMEM((seq_len, D), wide),
+        pltpu.VMEM((fsdp_size, 8, rows), wide),
+        pltpu.VMEM((fsdp_size - 1, 8, rows), wide),
+        pltpu.VMEM((4, 8, rows), wide),
+    ]
+    scratch += [dma((2, 4, 5))] + [dma((4, hops))] * 10 + [dma((4,))] * 2 + [dma((fsdp_size - 1,))] * 2
+    scratch += [dma((count,))] * 2 + [dma((count, 2, 2))] * 2 + [dma((count, 2))] * 2
+    scratch += [dma((count, 2, hops))] * 2 + [dma((count, 2, 2))] * 2 + [dma((count, 2))] * 2
+    scratch += [dma((count, 2))] + [dma((fsdp_size - 1,))] * 2 + [dma((3,))] * 2
+    scratch += [dma((4, 4)), pltpu.SemaphoreType.REGULAR]
+    return pl.pallas_call(
+        functools.partial(layer_kernel, fsdp_size, chunks),
+        out_shape=[shape((a.shape[0] * fsdp_size, a.shape[1]), low) for a in shards]
+        + [shape(w.shape, low) for w in by_need]
+        + [shape((seq_len, D), low)] * 2
+        + [shape((8, rows), wide)],
+        in_specs=[smem, vmem, vmem] + [hbm] * 5,
+        out_specs=[hbm] * 8 + [vmem] * 3,
+        scratch_shapes=scratch,
+        compiler_params=pltpu.CompilerParams(
+            collective_id=0, has_side_effects=True, vmem_limit_bytes=67043328
+        ),
+        name="layer_step",
+    )(length, scenes, cotangent, *shards, small)
+
+
+def on_device_wide(
     scenes_in,
     scene_lengths,
     cotangent,
@@ -256,6 +988,47 @@
     )
 
 
+def on_device(
+    scenes_in,
+    scene_lengths,
+    cotangent,
+    qkv_weight,
+    out_weight,
+    up_weight,
+    down_weight,
+    gain_one,
+    bias_one,
+    gain_two,
+    bias_two,
+):
+    rows = gain_one.shape[0]
+    fsdp_size = D // rows
+    small = jnp.stack([gain_one, bias_one, gain_two, bias_two])
+    small = jnp.pad(small, ((0, 12), (0, 0)))
+    results = layer_step(
+        fsdp_size,
+        scene_lengths,
+        scenes_in[0],
+        cotangent[0],
+        (qkv_weight, out_weight, up_weight, down_weight),
+        small,
+    )
+    down_sum, up_sum, out_sum, qkv_sum, layer_out, input_grad, small_sum = results[4:]
+    wide = jnp.float32
+    return (
+        layer_out[None],
+        input_grad[None],
+        qkv_sum.astype(wide),
+        out_sum.astype(wide),
+        up_sum.astype(wide),
+        down_sum.astype(wide),
+        small_sum[0],
+        small_sum[1],
+        small_sum[2],
+        small_sum[3],
+    )
+
+
 def solution(mesh):
     placed = (
         P(("dp", "fsdp"), None, None),
@@ -270,8 +1043,9 @@
         P("fsdp"),
         P("fsdp"),
     )
+    body = on_device if mesh.shape["dp"] == 4 and mesh.shape["fsdp"] == 8 else on_device_wide
     return jax.shard_map(
-        on_device,
+        body,
         mesh=mesh,
         in_specs=placed,
         out_specs=(

time: 906 us -> 286 us (0.32)
  waiting for transfers between devices: 687 us -> 0 us
  Pallas kernels: 0 us -> 273 us
  matrix products: 85.6 us -> 0 us
  blocking collectives: 79.8 us -> 0 us
  other arithmetic: 27.9 us -> 8.62 us
  between operations: 15.4 us -> 1.31 us
    reduce_scatter x4 -> x0, waiting for transfers between devices: 469 us -> none  [the longest x1 167 us: on_device(): lax.psum_scatter(up_grad, 'fsdp', scatter_dimension=0, tiled=True)]
    pallas_call x0 -> x1, Pallas kernels: none -> 273 us  [layer_step(): pl.pallas_call(functools.partial(layer_kernel, fsdp_size, chunks), out_sh...]
    all_gather x4 -> x0, waiting for transfers between devices: 184 us -> none  [the longest x1 80.4 us: on_device(): lax.all_gather(up_weight, 'fsdp', axis=0, tiled=True)]
    dot_general x18 -> x0, matrix products: 85.6 us -> none  [the longest x4 29.1 us: inner_rows(): lax.dot_general(left, right, (((0,), (0,)), ((), ())), preferred_element_...]
    all_gather x4 -> x0, blocking collectives: 43.6 us -> none  [the longest x1 13.6 us: on_device(): lax.all_gather(gain_one, 'fsdp', axis=0, tiled=True)]
    psum x1 -> x0, waiting for transfers between devices: 30.7 us -> none  [on_device(): lax.psum(shares[0].astype(jnp.bfloat16), 'dp').astype(jnp.float32)]
    unnamed x1 -> x0, blocking collectives: 25.9 us -> none
    convert_element_type x19 -> x4, other arithmetic: 20.5 us -> 7.31 us  [the longest x1 2.43 us: on_device(): qkv_sum.astype(wide)]
  transfers between devices with their start and end apart: 9 -> 0, of which waited for: 9 -> 0; matrix products, arithmetic and copies ran while one was open for 10% -> 0% of each run, Pallas kernels for 0% -> 0%
where the time goes in v2:
time: 286 us
  Pallas kernels  273 us (95%)
  other arithmetic  8.62 us (3%)
  local copies, waits for them, and re-layouts  2.95 us (1%)
    pallas_call x1, Pallas kernels, layer_step(): pl.pallas_call(functools.partial(layer_kernel, fsdp_size, chunks), out_sh...  273 us

profile of v2, /device:TPU:0, one launch (start us, length us, event | category | flops | bytes accessed | tf_op | source)
XLA Modules:
  0.0 286.2 jit_solution(5799124128284234134)
XLA Ops:
  1.3 1.3 fusion.6.refs_7_
  2.6 273.3 %layer_step.1 = (bf16[1024,3072]{1,0:T(8,128)(2,1)}, bf16[1024,1024]{1,0:T(8,128)(2,1)}, bf16[1024,4096]{1,0:T(8,128)(2,1)}, bf16[4096,1024]{1,0:T(8,128)(2,1)},...) custom-call(s32[1]{0:T(128)S(6)} %copy.23.refs_0_, ...), custom_call_target="tpu_custom_call" | custom-call | tf_op jit(solution)/shard_map/layer_step/pallas_call | solution.py:885
  275.9 0.0 copy-start.1
  275.9 1.3 slice_bitcast_fusion
  277.3 1.8 convert_element_type.15
  279.1 2.4 convert_element_type.14
  281.5 0.0 copy-done.1
  281.5 0.0 copy-start
  281.5 1.5 convert_element_type.16
  283.0 0.0 copy-done
  283.0 0.0 copy-start.3
  283.0 0.0 copy-start.2
  283.0 1.6 convert_element_type.17
  284.6 0.0 copy-done.3
  284.6 0.8 copy.24
  285.4 0.0 copy-done.2
  285.4 0.8 copy.25
Async XLA Ops:
  275.9 5.6 %copy-start.1 = (bf16[128,4096]{1,0:T(8,128)(2,1)S(1)}, bf16[128,4096]{1,0:T(8,128)(2,1)}, u32[]{:S(2)}) copy-start(bf16[128,4096]{1,0:T(8,128)(2,1)} %get-tuple-element.21) | copy-start | bytes 3145732
  281.5 1.5 copy-start
  283.0 1.6 copy-start.3
  283.0 2.4 copy-start.2

commit v3 on v2

--- a/solution.py
+++ b/solution.py
@@ -286,7 +286,7 @@
         send(view, view, ac.at[piece], bc.at[piece], c_peer).start()
 
     def source(k):
-        return lax.rem(place - k + column, column)
+        return place ^ k
 
     def from_column(piece, k):
         at = (piece, k - 1)
@@ -478,7 +478,7 @@
             mine = sum_b[i].at[d * 2 + half]
             add_into(mine, two_b[i].at[half])
             for k in range(1, column):
-                to = lax.rem(place + k, column)
+                to = place ^ k
                 go(
                     send(
                         mine.at[aligned(to, high)],
@@ -581,7 +581,7 @@
                     block(piece, place, d),
                     az.at[piece, k - 1],
                     bz.at[piece, k - 1],
-                    (d, lax.rem(place + k, column) * 2 + core),
+                    (d, (place ^ k) * 2 + core),
                 )
             )
         own = fulls[piece].at[aligned(f, rows)]
@@ -898,6 +898,61 @@
     )(length, scenes, cotangent, *shards, small)
 
 
+def widen_kernel(parts, *refs):
+    count = len(parts)
+    small = refs[6]
+    outs, small_outs = refs[7:13], refs[13:17]
+    stages, wides = refs[17 : 17 + count], refs[17 + count : 17 + 2 * count]
+    in_sem, out_sem = refs[17 + 2 * count :]
+    copies = []
+    for n, (which, at) in enumerate(parts):
+        copies.append(pltpu.make_async_copy(refs[which].at[at], stages[n], in_sem.at[n]))
+        copies[n].start()
+    for row, out in enumerate(small_outs):
+        out[...] = small[row]
+    backs = []
+    for n, (which, at) in enumerate(parts):
+        copies[n].wait()
+        source = stages[n]
+        if outs[which].dtype != source.dtype:
+            wides[n][...] = source[...].astype(jnp.float32)
+            source = wides[n]
+        backs.append(pltpu.make_async_copy(source, outs[which].at[at], out_sem.at[n]))
+        backs[n].start()
+    for copy in backs:
+        copy.wait()
+
+
+def widen(sums, rows, small):
+    low, wide = jnp.bfloat16, jnp.float32
+    parts, stages, wides = [], [], []
+    for which, array in enumerate((*sums, *rows)):
+        high, span = array.shape
+        step = max(16, min(high, 1 << ((BLOCK // span).bit_length() - 1)))
+        for row in range(0, high, step):
+            parts.append((which, pl.ds(row, step)))
+            stages.append(pltpu.VMEM((step, span), low))
+            wides.append(pltpu.VMEM((step, span) if which < len(sums) else (8, 128), wide))
+    shape = jax.ShapeDtypeStruct
+    hbm = pl.BlockSpec(memory_space=pltpu.HBM)
+    vmem = pl.BlockSpec(memory_space=pltpu.VMEM)
+    dma = pltpu.SemaphoreType.DMA
+    return pl.pallas_call(
+        functools.partial(widen_kernel, parts),
+        out_shape=[shape(a.shape, wide) for a in sums]
+        + [shape(a.shape, low) for a in rows]
+        + [shape((small.shape[1],), wide)] * 4,
+        in_specs=[hbm] * 6 + [vmem],
+        out_specs=[hbm] * 6 + [vmem] * 4,
+        scratch_shapes=stages + wides + [dma((len(parts),))] * 2,
+        compiler_params=pltpu.CompilerParams(vmem_limit_bytes=67043328),
+        name="widen",
+    )(*sums, *rows, small)
+
+
+BLOCK = 131072
+
+
 def on_device_wide(
     scenes_in,
     scene_lengths,
@@ -1014,19 +1069,8 @@
         small,
     )
     down_sum, up_sum, out_sum, qkv_sum, layer_out, input_grad, small_sum = results[4:]
-    wide = jnp.float32
-    return (
-        layer_out[None],
-        input_grad[None],
-        qkv_sum.astype(wide),
-        out_sum.astype(wide),
-        up_sum.astype(wide),
-        down_sum.astype(wide),
-        small_sum[0],
-        small_sum[1],
-        small_sum[2],
-        small_sum[3],
-    )
+    wide = widen((qkv_sum, out_sum, up_sum, down_sum), (layer_out, input_grad), small_sum)
+    return (wide[4][None], wide[5][None], *wide[:4], *wide[6:])
 
 
 def solution(mesh):

time: 286 us -> 273 us (0.955)
  other arithmetic: 8.62 us -> 1.31 us
  Pallas kernels: 273 us -> 270 us
  local copies, waits for them, and re-layouts: 2.95 us -> 0 us
    pallas_call x1, Pallas kernels: 273 us -> 265 us  [layer_step(): pl.pallas_call(functools.partial(layer_kernel, fsdp_size, chunks), out_sh...]
    convert_element_type x4 -> x0, other arithmetic: 7.31 us -> none  [the longest x1 2.43 us: on_device(): qkv_sum.astype(wide)]
    pallas_call x0 -> x1, Pallas kernels: none -> 5.42 us  [widen(): pl.pallas_call(functools.partial(widen_kernel, parts), out_shape=[shape(a...]
where the time goes in v3:
time: 273 us
  Pallas kernels  270 us (99%)
    pallas_call x1, Pallas kernels, layer_step(): pl.pallas_call(functools.partial(layer_kernel, fsdp_size, chunks), out_sh...  265 us

profile of v3, /device:TPU:0, one launch (start us, length us, event | category | flops | bytes accessed | tf_op | source)
XLA Modules:
  0.0 273.1 jit_solution(14752638845453571803)
XLA Ops:
  1.3 1.3 fusion.6.refs_7_
  2.6 264.9 %layer_step.1 = (bf16[1024,3072]{1,0:T(8,128)(2,1)}, bf16[1024,1024]{1,0:T(8,128)(2,1)}, bf16[1024,4096]{1,0:T(8,128)(2,1)}, bf16[4096,1024]{1,0:T(8,128)(2,1)},...) custom-call(s32[1]{0:T(128)S(6)} %copy.21.refs_0_, ...), custom_call_target="tpu_custom_call" | custom-call | tf_op jit(solution)/shard_map/layer_step/pallas_call | solution.py:885
  267.5 5.4 %widen.1 = (f32[128,3072]{1,0:T(8,128)}, f32[128,1024]{1,0:T(8,128)}, f32[128,4096]{1,0:T(8,128)}, f32[512,1024]{1,0:T(8,128)}, bf16[256,1024]{1,0:T(8,128)(2,1)...) custom-call(bf16[128,3072]{1,0:T(8,128)(2,1)} %get-tuple-element.27.refs_0_, ...), custom_call_target="tpu_custom_call" | custom-call | tf_op jit(solution)/shard_map/widen/pallas_call | solution.py:940

commit v4 on v3

--- a/solution.py
+++ b/solution.py
@@ -528,10 +528,11 @@
 
     stages = (first, second, last, spread, finish)
     order = []
-    for step in range(count + len(stages) - 1):
-        for n, stage in enumerate(stages):
-            if 0 <= step - n < count:
-                order.append((stage, step - n))
+    lags = (0, 2, 3, 4, 5)
+    for step in range(count + lags[-1]):
+        for stage, lag in zip(stages, lags):
+            if 0 <= step - lag < count:
+                order.append((stage, step - lag))
     done = []
     waiting = []
     paired = []
@@ -542,8 +543,11 @@
             pair(i)
             paired.append(i)
 
+    owed = [0]
+
     def advance(limit):
-        for _ in range(limit):
+        steps, owed[0] = divmod(owed[0] + limit, 2)
+        for _ in range(steps):
             if len(done) < len(order) and order[len(done)][1] in paired:
                 stage, i = order[len(done)]
                 done.append(1)
@@ -820,7 +824,7 @@
     for k in range(1, 4):
         arrived(small_b.at[d ^ k], us.at[k - 1], ur.at[k - 1], c_peer)
     small_out[...] = (small_b[0] + small_b[1]) + (small_b[2] + small_b[3])
-    pump(len(order))
+    pump(2 * len(order))
     for copy in pending:
         copy.wait_send()
     for i in range(max(0, count - slots_other), count):

time: 273 us -> 264 us (0.967)
  Pallas kernels: 270 us -> 261 us
    pallas_call x1, Pallas kernels: 265 us -> 256 us  [layer_step(): pl.pallas_call(functools.partial(layer_kernel, fsdp_size, chunks), out_sh...]
where the time goes in v4:
time: 264 us
  Pallas kernels  261 us (99%)
    pallas_call x1, Pallas kernels, layer_step(): pl.pallas_call(functools.partial(layer_kernel, fsdp_size, chunks), out_sh...  256 us
    pallas_call x1, Pallas kernels, widen(): pl.pallas_call(functools.partial(widen_kernel, parts), out_shape=[shape(a...  5.42 us

profile of v4, /device:TPU:0, one launch (start us, length us, event | category | flops | bytes accessed | tf_op | source)
XLA Modules:
  0.0 263.9 jit_solution(534371711876602942)
XLA Ops:
  1.3 1.3 fusion.6.refs_7_
  2.6 255.6 %layer_step.1 = (bf16[1024,3072]{1,0:T(8,128)(2,1)}, bf16[1024,1024]{1,0:T(8,128)(2,1)}, bf16[1024,4096]{1,0:T(8,128)(2,1)}, bf16[4096,1024]{1,0:T(8,128)(2,1)},...) custom-call(s32[1]{0:T(128)S(6)} %copy.21.refs_0_, ...), custom_call_target="tpu_custom_call" | custom-call | tf_op jit(solution)/shard_map/layer_step/pallas_call | solution.py:889
  258.2 5.4 %widen.1 = (f32[128,3072]{1,0:T(8,128)}, f32[128,1024]{1,0:T(8,128)}, f32[128,4096]{1,0:T(8,128)}, f32[512,1024]{1,0:T(8,128)}, bf16[256,1024]{1,0:T(8,128)(2,1)...) custom-call(bf16[128,3072]{1,0:T(8,128)(2,1)} %get-tuple-element.27.refs_0_, ...), custom_call_target="tpu_custom_call" | custom-call | tf_op jit(solution)/shard_map/widen/pallas_call | solution.py:944

commit v5 on v4

--- a/solution.py
+++ b/solution.py
@@ -546,7 +546,7 @@
     owed = [0]
 
     def advance(limit):
-        steps, owed[0] = divmod(owed[0] + limit, 2)
+        steps, owed[0] = divmod(owed[0] + limit, 3)
         for _ in range(steps):
             if len(done) < len(order) and order[len(done)][1] in paired:
                 stage, i = order[len(done)]
@@ -824,7 +824,7 @@
     for k in range(1, 4):
         arrived(small_b.at[d ^ k], us.at[k - 1], ur.at[k - 1], c_peer)
     small_out[...] = (small_b[0] + small_b[1]) + (small_b[2] + small_b[3])
-    pump(2 * len(order))
+    pump(3 * len(order))
     for copy in pending:
         copy.wait_send()
     for i in range(max(0, count - slots_other), count):

time: 264 us -> 273 us (1.034)
  Pallas kernels: 261 us -> 270 us
    pallas_call x1, Pallas kernels: 256 us -> 264 us  [layer_step(): pl.pallas_call(functools.partial(layer_kernel, fsdp_size, chunks), out_sh...]
where the time goes in v5:
time: 273 us; the launch traced here: 272 us
  Pallas kernels  270 us (99%)
    pallas_call x1, Pallas kernels, layer_step(): pl.pallas_call(functools.partial(layer_kernel, fsdp_size, chunks), out_sh...  264 us

profile of v5, /device:TPU:0, one launch (start us, length us, event | category | flops | bytes accessed | tf_op | source)
XLA Modules:
  0.0 272.4 jit_solution(15712481613712738905)
XLA Ops:
  1.3 1.3 fusion.6.refs_7_
  2.6 264.2 %layer_step.1 = (bf16[1024,3072]{1,0:T(8,128)(2,1)}, bf16[1024,1024]{1,0:T(8,128)(2,1)}, bf16[1024,4096]{1,0:T(8,128)(2,1)}, bf16[4096,1024]{1,0:T(8,128)(2,1)},...) custom-call(s32[1]{0:T(128)S(6)} %copy.21.refs_0_, ...), custom_call_target="tpu_custom_call" | custom-call | tf_op jit(solution)/shard_map/layer_step/pallas_call | solution.py:889
  266.8 5.4 %widen.1 = (f32[128,3072]{1,0:T(8,128)}, f32[128,1024]{1,0:T(8,128)}, f32[128,4096]{1,0:T(8,128)}, f32[512,1024]{1,0:T(8,128)}, bf16[256,1024]{1,0:T(8,128)(2,1)...) custom-call(bf16[128,3072]{1,0:T(8,128)(2,1)} %get-tuple-element.27.refs_0_, ...), custom_call_target="tpu_custom_call" | custom-call | tf_op jit(solution)/shard_map/widen/pallas_call | solution.py:944
